TPU v7x, 32 devices: a whole 2x2x4 slice. The times are simulated.
32 devices in a mesh: scene: 4 (over x, core), brick: 8 (over z, y).
Axes of the slice: x: 2, y: 2, z: 4, core: 2. Of those that a mesh axis runs over, the one named last changes fastest.
Arguments:
- features: bfloat16 [4, 4096, 64], P('scene', 'brick'), may hold values from -6 to 6
- cotangent: bfloat16 [4, 4096, 64], P('scene', 'brick'), may hold values from -6 to 6
- first_weight: bfloat16 [1728, 64], replicated, may hold values from -0.15625 to 0.15625
- second_weight: bfloat16 [1728, 64], replicated, may hold values from -0.15625 to 0.15625
- send_rows: int32 [4, 1024], P('scene', 'brick'), may hold values from 0 to 512, as said below
- gather_rows: int32 [4, 8000], P('scene', 'brick'), may hold values from 0 to 640, as said below
Outputs:
- output: bfloat16 [4, 4096, 64], P('scene', 'brick')
- grad_input: bfloat16 [4, 4096, 64], P('scene', 'brick')
- grad_first: float32 [1728, 64], replicated
- grad_second: float32 [1728, 64], replicated
Inputs may be any that keep to these rules, and one draw needn't show every extreme that they name: `send_rows`: entries equal to 512 are empty slots; used entries come first in each half and name voxels on the face of active bricks towards that neighbour; in every draw some pair of neighbouring indices sends all 64 rows to each other. Index 0 sends nothing down, the last index nothing up. `gather_rows`: row 640 is the zero row; inactive slots read only it; rows 512 and up read boundary rows in the order of the neighbour's send list. Every index of brick holds exactly one active brick slot, and bricks touch only bricks of the same or an adjacent index.
All inputs are finite; a program needn't handle non-finite values.
Results may differ from a plain program's by a relative error of at most 0.0059.
Values may be sent and summed in bfloat16 or wider, within the bound.
No kernel may reach another device: no remote copies, remote signals or barrier semaphores. Data moves between devices by JAX's collectives and lax.ppermute only.
A program may use at most 64 MiB of HBM per device.

v0:
```python
import jax
import jax.numpy as jnp
from jax import lax
from jax.experimental import pallas as pl
from jax.experimental.pallas import tpu as pltpu
from jax.sharding import PartitionSpec as P

F32 = jnp.float32
BF16 = jnp.bfloat16

E = 8
C = 64
FACE = E * E
VOX = E * FACE
RIM = E + 2
CELLS = 3 * RIM * E
BOTH = ("scene", "brick")

PAIRS = (
    ((0, 0), (0, 1)),
    ((1, 0), (1, 1)),
    ((2, 0), (2, 1)),
    ((0, 2), (1, 2)),
    ((2, 2), None),
)
TILES = len(PAIRS)
KDIM = TILES * 2 * C
LOW, OWN, HIGH = 0, 6, 16
PLANES = 20
WIDE = 4
SPAN = 2

LIMIT = pltpu.CompilerParams(vmem_limit_bytes=24 << 20)
VMEM_SPEC = pl.BlockSpec(memory_space=pltpu.VMEM)
SMEM_SPEC = pl.BlockSpec(memory_space=pltpu.SMEM)


def sigmoid(v):
    return jax.nn.sigmoid(v)


def slope(v):
    s = sigmoid(v)
    return s * (1.0 + v * (1.0 - s))


def low_lanes(shape):
    return lax.broadcasted_iota(jnp.int32, shape, len(shape) - 1) % (2 * C) < C


def weight_kernel(w1_ref, w2_ref, f1_ref, f2_ref, b1_ref, b2_ref):
    zero = jnp.zeros((C, C), BF16)
    for w_ref, f_ref, b_ref in ((w1_ref, f1_ref, b1_ref), (w2_ref, f2_ref, b2_ref)):
        blocks = [w_ref[:, o * C : (o + 1) * C] for o in range(27)]
        for t, pair in enumerate(PAIRS):
            for k, a in enumerate((0, 1, 2, 2)):
                halves = [zero if bc is None else blocks[9 * a + 3 * bc[0] + bc[1]] for bc in pair]
                f_ref[k * C : (k + 1) * C, t * 2 * C : (t + 1) * 2 * C] = jnp.concatenate(halves, axis=1)
            for h, bc in enumerate(pair):
                rows = slice((2 * t + h) * C, (2 * t + h + 1) * C)
                if bc is None:
                    b_ref[rows, :] = jnp.zeros((C, 4 * C), BF16)
                    continue
                o = 26 - 3 * bc[0] - bc[1]
                b_ref[rows, 0 : 2 * C] = jnp.concatenate([blocks[o], blocks[o - 9]], axis=1)
                b_ref[rows, 2 * C : 4 * C] = jnp.concatenate([blocks[o - 18], blocks[o - 18]], axis=1)


def prepare_weights(w1, w2):
    fwd = jax.ShapeDtypeStruct((4 * C, KDIM), BF16)
    bwd = jax.ShapeDtypeStruct((KDIM, 4 * C), BF16)
    return pl.pallas_call(
        weight_kernel,
        out_shape=(fwd, fwd, bwd, bwd),
        in_specs=[VMEM_SPEC] * 2,
        out_specs=(VMEM_SPEC,) * 4,
        compiler_params=LIMIT,
        cost_estimate=pl.CostEstimate(flops=0, bytes_accessed=2 << 20, transcendentals=0),
    )(w1, w2)


def rim_spread(first):
    lane = lax.broadcasted_iota(jnp.int32, (2 * C, 4 * C), 1)
    c = jnp.where(lane >= RIM * E, 1, 0) + jnp.where(lane >= 2 * RIM * E, 1, 0)
    cell = lane - c * (RIM * E)
    source = (cell >> 3) * RIM + (cell & (E - 1)) + c + first
    return jnp.where(lax.broadcasted_iota(jnp.int32, (2 * C, 4 * C), 0) == source, 1.0, 0.0).astype(BF16)


def pack_kernel(even_ref, feat_ref, cot_ref, send_ref, gather_ref, first_ref, second_ref, codes_ref):
    send = send_ref[...]
    upper = lax.broadcasted_iota(jnp.int32, send.shape, 1) >= FACE
    row = jnp.where(upper, send - (VOX - FACE), send)
    sent = jnp.where((row >= 0) & (row < FACE), row + 1, 0)
    slot = gather_ref[:, : 2 * C] - VOX
    bottom = jnp.where((slot >= 0) & (slot < FACE), slot + FACE + 1, 0)
    slot = gather_ref[:, -2 * C :] - (VOX + FACE)
    top = jnp.where((slot >= 0) & (slot < FACE), slot + 1, 0)

    def spread(cells, first):
        wide = jnp.broadcast_to(cells.astype(F32), (E, 2 * C)).astype(BF16)
        v = jnp.dot(wide, rim_spread(first), preferred_element_type=F32)
        return [v[:1, : 2 * C], v[:1, 2 * C :]]

    rows = [sent.astype(F32)] + spread(bottom, 0) + spread(top, 2 * C - RIM * RIM)
    codes = jnp.concatenate(rows + [jnp.zeros((E - len(rows), 2 * C), F32)], axis=0).astype(BF16)
    codes_ref[...] = codes
    even = even_ref[0] == 1

    def put(ref, upward):
        at = 0
        for source, layers in ((feat_ref, WIDE), (cot_ref, SPAN)):
            start = VOX - layers * FACE if upward else 0
            for lane in range(start, start + layers * FACE, 2 * C):
                ref[at : at + C, :] = source[0, :, lane : lane + 2 * C]
                at += C
        ref[at : at + E, :] = codes

    @pl.when(even)
    def _():
        put(first_ref, True)
        put(second_ref, False)

    @pl.when(jnp.logical_not(even))
    def _():
        put(first_ref, False)
        put(second_ref, True)


def pack(even, feat, cot, send, gather):
    rows = (WIDE + SPAN) * FACE * C // (2 * C) + E
    return pl.pallas_call(
        pack_kernel,
        out_shape=(jax.ShapeDtypeStruct((rows, 2 * C), BF16),) * 2
        + (jax.ShapeDtypeStruct((E, 2 * C), BF16),),
        in_specs=[SMEM_SPEC] + [VMEM_SPEC] * 4,
        out_specs=(VMEM_SPEC,) * 3,
        compiler_params=LIMIT,
    )(even, feat, cot, send, gather)


def z_shifted(v):
    axis = v.ndim - 2
    z = lax.broadcasted_iota(jnp.int32, v.shape, axis)
    before = jnp.where(z == 0, 0.0, pltpu.roll(v, 1, axis))
    after = jnp.where(z == E - 1, 0.0, pltpu.roll(v, E - 1, axis))
    return jnp.where(low_lanes(v.shape), before, v), after


def rim_cells(pick, plane):
    m = jnp.dot(pick, plane.reshape(FACE, 2 * C).astype(BF16), preferred_element_type=F32)
    m = m.reshape(3, RIM, E, 2 * C)
    return jnp.where(low_lanes(m.shape[1:]), m[0], m[1]), m[2]


def pick_matrix(send_codes, cell_codes):
    row = lax.broadcasted_iota(jnp.int32, (FACE, 2 * C), 0).astype(F32) + 1.0
    listed = jnp.where(row == send_codes, 1.0, 0.0).astype(BF16)
    slot = lax.broadcasted_iota(jnp.int32, (2 * C, 4 * C), 0).astype(F32) + 1.0
    cells = jnp.concatenate([cell_codes[0:1], cell_codes[1:2]], axis=1)
    read = jnp.where(slot == cells, 1.0, 0.0).astype(BF16)
    picked = jnp.dot(listed, read, preferred_element_type=F32)
    return jnp.transpose(picked)[:CELLS].astype(BF16)


def stack_x(planes):
    count = planes.shape[0] // E
    v = planes.reshape(count, E, E, 2 * C)
    return jnp.stack([v[:, y] for y in range(E)], axis=0)


def x_taps(r, first, count):
    here = slice(first, first + count)
    prev = slice(first - 1, first + count - 1)
    after = slice(first + 1, first + count + 1)
    v0 = r[..., : 2 * C]
    v1 = r[..., 2 * C :]
    s = jnp.where(low_lanes((E, count, E, 2 * C)), v0[:, prev], v0[:, here])
    return s + pltpu.roll(s, C, 3) + v1[:, after]


def put_rows(out_ref, v):
    rows = jnp.stack([v[:, x] for x in range(E)], axis=0).reshape(VOX, 2 * C)
    out_ref[0] = jnp.transpose(rows)[:C].astype(BF16)


def put_interior(q_ref, first, v):
    count = v.shape[1]
    rows = pl.ds(first * E, count * E)
    z0, z1 = z_shifted(v)
    z0 = z0.reshape(E, count * E, 2 * C).astype(BF16)
    zero = jnp.zeros((1, count, E, 2 * C), F32)
    pair = jnp.where(low_lanes(v.shape), jnp.concatenate([zero, z1[: E - 1]], axis=0), z1)
    pair = pair.reshape(E, count * E, 2 * C).astype(BF16)
    z1 = z1.reshape(E, count * E, 2 * C).astype(BF16)
    none = jnp.zeros((count * E, 2 * C), BF16)
    for y in range(E):
        q_ref[y, rows, 0 : 2 * C] = z0[y - 1] if y > 0 else none
        q_ref[y, rows, 2 * C : 4 * C] = z0[y]
        q_ref[y, rows, 4 * C : 6 * C] = z0[y + 1] if y < E - 1 else none
        q_ref[y, rows, 6 * C : 8 * C] = pair[y]
        q_ref[y, rows, 8 * C : 10 * C] = z1[y + 1] if y < E - 1 else none


def put_rims(q_ref, first, rims):
    count = len(rims)
    rows = pl.ds(first * E, count * E)
    z0 = jnp.stack([r[0] for r in rims], axis=1)
    z1 = jnp.stack([r[1] for r in rims], axis=1)
    pair = jnp.where(low_lanes(z1[:-1].shape), z1[:-1], z1[1:])
    z0 = z0.reshape(RIM, count * E, 2 * C).astype(BF16)
    z1 = z1.reshape(RIM, count * E, 2 * C).astype(BF16)
    pair = pair.reshape(RIM - 1, count * E, 2 * C).astype(BF16)
    for y in range(E):
        for b in range(3):
            q_ref[y, rows, b * 2 * C : (b + 1) * 2 * C] = z0[y + b]
        q_ref[y, rows, 6 * C : 8 * C] = pair[y]
        q_ref[y, rows, 8 * C : 10 * C] = z1[y + 2]


def fill(q_ref, low, own, high, picks):
    low_pick, below_pick, above_pick, high_pick = picks
    put_interior(q_ref, OWN, own)
    put_interior(q_ref, LOW, low)
    put_interior(q_ref, HIGH, high)
    put_rims(
        q_ref,
        OWN - 2,
        [rim_cells(low_pick, own[:, 0]), rim_cells(below_pick, low[:, -1])],
    )
    put_rims(
        q_ref,
        OWN + E,
        [rim_cells(above_pick, high[:, 0]), rim_cells(high_pick, own[:, -1])],
    )


def main_kernel(
    even_ref,
    feat_ref,
    cot_ref,
    first_ref,
    second_ref,
    codes_ref,
    f1_ref,
    f2_ref,
    b2_ref,
    out_ref,
    grad_ref,
    delta_ref,
    pick_ref,
    q1_ref,
    q2_ref,
    q3_ref,
):
    even = even_ref[0] == 1
    first = first_ref[...]
    second = second_ref[...]
    upper = jnp.where(even, first, second).astype(F32)
    lower = jnp.where(even, second, first).astype(F32)

    def planes(t):
        return stack_x(jnp.transpose(jnp.concatenate([t, t], axis=0)).reshape(-1, E, 2 * C))

    def parts(packed):
        blocks = [packed[k * C : (k + 1) * C] for k in range((WIDE + SPAN) // 2)]
        codes = packed[len(blocks) * C :]
        f = jnp.concatenate(blocks[: WIDE // 2], axis=1)
        c = jnp.concatenate(blocks[WIDE // 2 :], axis=1)
        return planes(f), planes(c), codes

    low_f, low_c, low_codes = parts(lower)
    high_f, high_c, high_codes = parts(upper)
    codes = codes_ref[...].astype(F32)
    own_f = planes(feat_ref[0].astype(F32))
    own_c = planes(cot_ref[0].astype(F32))

    picks = (
        pick_matrix(codes[0:1], low_codes[3:5]),
        pick_matrix(low_codes[0:1], codes[1:3]),
        pick_matrix(high_codes[0:1], codes[3:5]),
        pick_matrix(codes[0:1], high_codes[1:3]),
    )
    pick_ref[0] = picks[1]
    pick_ref[1] = picks[2]

    def conv(q_ref, w, flipped=False):
        q = q_ref[...].reshape(E * PLANES * E, KDIM)
        dims = (((1,), (0 if flipped else 1,)), ((), ()))
        r = lax.dot_general(q, w, dims, preferred_element_type=F32)
        return r.reshape(E, PLANES, E, 4 * C)

    def rounded(v):
        return v.astype(BF16).astype(F32)

    def weight_gradient(which, q_ref, delta):
        zero = jnp.zeros((E, 1, E, 2 * C), F32)
        d = jnp.concatenate([zero, zero, delta, zero, zero, zero], axis=1)
        n = E + 4
        before = jnp.concatenate([zero, d[:, : n - 1]], axis=1)
        d0 = jnp.where(low_lanes((E, n, E, 2 * C)), d[:, 1 : n + 1], d[:, :n])
        d1 = before
        rows = E * n * E
        d0 = jnp.transpose(d0.reshape(rows, 2 * C)).astype(BF16)
        d1 = jnp.transpose(d1.reshape(rows, 2 * C))[:C].astype(BF16)
        dt = jnp.concatenate([d0, d1], axis=0)
        q = q_ref[:, (OWN - 2) * E : (OWN + E + 2) * E, :].reshape(rows, KDIM)
        g = jnp.dot(dt, q, preferred_element_type=F32).astype(BF16)
        for t in range(TILES):
            grad_ref[which, t] = g[:, t * 2 * C : (t + 1) * 2 * C]

    fill(q1_ref, low_f, own_f, high_f, picks)
    r = conv(q1_ref, f1_ref[...])
    pre_low = x_taps(r, LOW + 1, WIDE - 1)
    pre_own = x_taps(r, OWN, E)
    pre_high = x_taps(r, HIGH, WIDE - 1)
    act = [rounded(v * sigmoid(v)) for v in (pre_low, pre_own, pre_high)]
    pad_plane = jnp.zeros((E, 1, E, 2 * C), F32)
    fill(
        q2_ref,
        jnp.concatenate([pad_plane, act[0]], axis=1),
        act[1],
        jnp.concatenate([act[2], pad_plane], axis=1),
        picks,
    )
    r = conv(q2_ref, f2_ref[...])
    second_own = x_taps(r, OWN, E)
    put_rows(out_ref, second_own * sigmoid(second_own))
    second_low = x_taps(r, LOW + WIDE - SPAN, SPAN)
    second_high = x_taps(r, HIGH, SPAN)
    delta_own = rounded(own_c * slope(second_own))
    delta_low = rounded(low_c * slope(second_low))
    delta_high = rounded(high_c * slope(second_high))
    weight_gradient(1, q2_ref, delta_own)
    pads = jnp.zeros((E, WIDE - SPAN, E, 2 * C), F32)
    fill(
        q3_ref,
        jnp.concatenate([pads, delta_low], axis=1),
        delta_own,
        jnp.concatenate([delta_high, pads], axis=1),
        picks,
    )
    r = conv(q3_ref, b2_ref[...], True)
    first_own = rounded(x_taps(r, OWN, E) * slope(pre_own))
    first_low = rounded(x_taps(r, LOW + WIDE - 1, 1) * slope(pre_low[:, -1:]))
    first_high = rounded(x_taps(r, HIGH, 1) * slope(pre_high[:, :1]))
    weight_gradient(0, q1_ref, first_own)
    delta = jnp.concatenate([first_low, first_own, first_high], axis=1)
    delta_ref[...] = delta.reshape(E, (E + 2) * E, 2 * C).astype(BF16)


def main_call(even, feat, cot, first, second, codes, f1, f2, b2):
    q_shape = pltpu.VMEM((E, PLANES * E, KDIM), BF16)
    return pl.pallas_call(
        main_kernel,
        out_shape=(
            jax.ShapeDtypeStruct(feat.shape, BF16),
            jax.ShapeDtypeStruct((2, TILES, 3 * C, 2 * C), BF16),
            jax.ShapeDtypeStruct((E, (E + 2) * E, 2 * C), BF16),
            jax.ShapeDtypeStruct((2, CELLS, FACE), BF16),
        ),
        in_specs=[SMEM_SPEC] + [VMEM_SPEC] * 8,
        out_specs=(VMEM_SPEC,) * 4,
        scratch_shapes=[q_shape] * 3,
        compiler_params=LIMIT,
        cost_estimate=pl.CostEstimate(flops=10**10, bytes_accessed=4 << 20, transcendentals=10**6),
    )(even, feat, cot, first, second, codes, f1, f2, b2)


def last_kernel(delta_ref, pick_ref, b1_ref, out_ref, q_ref):
    delta = delta_ref[...].astype(F32).reshape(E, E + 2, E, 2 * C)
    put_interior(q_ref, 2, delta[:, 1 : E + 1])
    below = rim_cells(pick_ref[0], delta[:, 0])
    above = rim_cells(pick_ref[1], delta[:, E + 1])
    put_rims(q_ref, 0, [below, below])
    put_rims(q_ref, E + 2, [above, above])
    q = q_ref[...].reshape(E * (E + 4) * E, KDIM)
    r = jnp.dot(q, b1_ref[...], preferred_element_type=F32)
    put_rows(out_ref, x_taps(r.reshape(E, E + 4, E, 4 * C), 2, E))


def last_call(delta, pick, b1, shape):
    return pl.pallas_call(
        last_kernel,
        out_shape=jax.ShapeDtypeStruct(shape, BF16),
        in_specs=[VMEM_SPEC] * 3,
        out_specs=VMEM_SPEC,
        scratch_shapes=[pltpu.VMEM((E, (E + 4) * E, KDIM), BF16)],
        compiler_params=LIMIT,
        cost_estimate=pl.CostEstimate(flops=10**9, bytes_accessed=2 << 20, transcendentals=0),
    )(delta, pick, b1)


def finish_kernel(scale, flag_ref, mine_ref, theirs_ref, g1_ref, g2_ref):
    swap = flag_ref[0] == 1
    mine, theirs = mine_ref[...], theirs_ref[...]
    for g_ref, one, two in ((g1_ref, mine, theirs), (g2_ref, theirs, mine)):
        total = jnp.where(swap, two, one).astype(F32) * scale
        for a in range(3):
            at = {}
            for t, pair in enumerate(PAIRS):
                for h, bc in enumerate(pair):
                    if bc is not None:
                        at[3 * bc[0] + bc[1]] = total[t, a * C : (a + 1) * C, h * C : (h + 1) * C]
            g_ref[:, 9 * a * C : 9 * (a + 1) * C] = jnp.concatenate([at[o] for o in range(9)], axis=1)


def finish(flag, mine, theirs, scale):
    shape = jax.ShapeDtypeStruct((C, 27 * C), F32)
    tiles = (TILES, 3 * C, 2 * C)
    return pl.pallas_call(
        lambda *refs: finish_kernel(scale, *refs),
        out_shape=(shape, shape),
        in_specs=[SMEM_SPEC] + [VMEM_SPEC] * 2,
        out_specs=(VMEM_SPEC,) * 2,
        compiler_params=LIMIT,
    )(flag, mine.reshape(tiles), theirs.reshape(tiles))


def xor_permute(v, scene_bits, brick_bits):
    bricks = lax.axis_size("brick")
    total = lax.axis_size("scene") * bricks
    pairs = [
        (i, ((i // bricks) ^ scene_bits) * bricks + ((i % bricks) ^ brick_bits)) for i in range(total)
    ]
    return lax.ppermute(v, BOTH, pairs)


def all_sum(v):
    scenes, bricks = lax.axis_size("scene"), lax.axis_size("brick")
    if scenes != 4 or bricks != 8:
        total = lax.psum(v.astype(F32), BOTH)
        return jnp.zeros((1,), jnp.int32), total[0], total[1]
    scene, brick = lax.axis_index("scene"), lax.axis_index("brick")
    core, across = scene & 1, scene >> 1
    where = across * 2 + (brick & 1)
    parts = v.reshape(2, 4, -1, 2 * C)

    def pick(array, index):
        return lax.dynamic_index_in_dim(array, index, 0, keepdims=False)

    def sum4(own, one, two, three):
        return (own.astype(F32) + one.astype(F32)) + (two.astype(F32) + three.astype(F32))

    other = xor_permute(pick(parts, 1 - core), 1, 0)
    chip = (pick(parts, core).astype(F32) + other.astype(F32)).astype(BF16)
    moved = [
        xor_permute(pick(chip, where ^ k), 2 * (k >> 1), k & 1) for k in (1, 2, 3)
    ]
    plane = sum4(pick(chip, where), *moved).astype(BF16)
    column = [xor_permute(plane, 0, 2 * k) for k in (1, 2, 3)]
    whole = sum4(plane, *column).astype(BF16)
    back = [xor_permute(whole, 2 * (k >> 1), k & 1) for k in (1, 2, 3)]
    mine = jnp.zeros(chip.shape, BF16)
    for k, piece in enumerate([whole] + back):
        mine = lax.dynamic_update_index_in_dim(mine, piece, where ^ k, 0)
    theirs = xor_permute(mine, 1, 0)
    return core[None], mine, theirs


def step(features, cotangent, first_weight, second_weight, send_rows, gather_rows):
    bricks = lax.axis_size("brick")
    even = 1 - (lax.axis_index("brick") & 1)[None]
    feat, cot = jnp.swapaxes(features, 1, 2), jnp.swapaxes(cotangent, 1, 2)

    first, second, codes = pack(even, feat, cot, send_rows, gather_rows)
    within = [(i, i ^ 1) for i in range(bricks) if i ^ 1 < bricks]
    between = [(i, ((i + 1) ^ 1) - 1) for i in range(1, bricks) if ((i + 1) ^ 1) - 1 < bricks]
    first = lax.ppermute(first, "brick", within)
    second = lax.ppermute(second, "brick", between)
    f1, f2, b1, b2 = prepare_weights(first_weight.T, second_weight.T)

    output, grads, delta, pick = main_call(even, feat, cot, first, second, codes, f1, f2, b2)
    grad_input = last_call(delta, pick, b1, feat.shape)
    flag, mine, theirs = all_sum(grads)
    scale = float(lax.axis_size("scene") * bricks * VOX) ** -0.5
    grad_first, grad_second = finish(flag, mine, theirs, scale)
    return jnp.swapaxes(output, 1, 2), jnp.swapaxes(grad_input, 1, 2), grad_first.T, grad_second.T


def solution(mesh):
    rows = P("scene", "brick", None)
    table = P("scene", "brick")
    return jax.shard_map(
        step,
        mesh=mesh,
        in_specs=(rows, rows, P(), P(), table, table),
        out_specs=(rows, rows, P(), P()),
        check_vma=False,
    )
```

profile of v0, /device:TPU:0, one launch (start us, length us, event | category | flops | bytes accessed | tf_op | source)
XLA Modules:
  0.0 48.5 jit_solution(8860202013951923557)
XLA Ops:
  0.6 0.0 copy-start.6
  0.6 0.0 copy-start.7
  0.7 0.7 %copy-done.6 = s32[1,1000]{1,0:T(1,128)S(1)} copy-done((s32[1,1000]{1,0:T(1,128)S(1)}, s32[1,1000]{1,0:T(1,128)}, u32[]{:S(2)}) %copy-start.6) | copy-done | bytes 4024
  1.3 0.0 copy-done.7
  1.3 0.0 copy-start.2
  1.3 0.8 %copy-done.2 = bf16[1,512,64]{1,2,0:T(8,128)(2,1)S(1)} copy-done((bf16[1,512,64]{1,2,0:T(8,128)(2,1)S(1)}, bf16[1,512,64]{1,2,0:T(8,128)(2,1)}, u32[]{:S(2)}) %copy-start.2) | copy-done | bytes 65560
  2.2 0.0 copy-start.4
  2.2 0.8 %copy-done.4 = bf16[1,512,64]{1,2,0:T(8,128)(2,1)S(1)} copy-done((bf16[1,512,64]{1,2,0:T(8,128)(2,1)S(1)}, bf16[1,512,64]{1,2,0:T(8,128)(2,1)}, u32[]{:S(2)}) %copy-start.4) | copy-done | bytes 65560
  3.0 0.2 shard_map.93
  3.2 3.1 %collective-permute-start = (bf16[200,128]{1,0:T(8,128)(2,1)S(1)}, bf16[200,128]{1,0:T(8,128)(2,1)S(1)}, u32[]{:S(2)}, u32[]{:S(2)}) collective-permute-start(bf16[200,128]{1,0:T(8,128)(2,1)S(1)} %get-tuple-element.17), channel_id=1, source_target_pairs={{0,1},{1,0},{2,3},{3,2},{4,5},{5,4},{6,7},{7,6},{8,9},{9,8},{10,11... | collective-permute-start | bytes 153608 | tf_op jit(solution)/shard_map/ppermute | solution.py:469
  6.3 0.7 %collective-permute-start.1 = (bf16[200,128]{1,0:T(8,128)(2,1)S(1)}, bf16[200,128]{1,0:T(8,128)(2,1)S(1)}, u32[]{:S(2)}, u32[]{:S(2)}) collective-permute-start(bf16[200,128]{1,0:T(8,128)(2,1)S(1)} %get-tuple-element.18), channel_id=1, source_target_pairs={{1,2},{2,1},{3,4},{4,3},{5,6},{6,5},{9,10},{10,9},{11,12},{12,11},... | collective-permute-start | bytes 153608 | tf_op jit(solution)/shard_map/ppermute | solution.py:470
  7.0 0.0 copy-start
  7.0 0.9 %copy-done = bf16[1728,64]{0,1:T(8,128)(2,1)S(1)} copy-done((bf16[1728,64]{0,1:T(8,128)(2,1)S(1)}, bf16[1728,64]{0,1:T(8,128)(2,1)}, u32[]{:S(2)}) %copy-start) | copy-done | bytes 221208
  7.9 0.0 copy-start.1
  7.9 0.9 %copy-done.1 = bf16[1728,64]{0,1:T(8,128)(2,1)S(1)} copy-done((bf16[1728,64]{0,1:T(8,128)(2,1)S(1)}, bf16[1728,64]{0,1:T(8,128)(2,1)}, u32[]{:S(2)}) %copy-start.1) | copy-done | bytes 221208
  8.8 0.0 copy-start.3
  8.8 0.0 copy-start.5
  8.8 0.2 shard_map.94
  9.0 0.0 collective-permute-done.first_ref
  9.0 0.0 collective-permute-done.1.second_ref
  9.1 0.6 %copy-done.3 = bf16[1,512,64]{1,2,0:T(8,128)(2,1)S(1)} copy-done((bf16[1,512,64]{1,2,0:T(8,128)(2,1)S(1)}, bf16[1,512,64]{1,2,0:T(8,128)(2,1)}, u32[]{:S(2)}) %copy-start.3) | copy-done | bytes 65560
  9.7 0.0 copy-done.5
  9.7 6.1 %shard_map.95 = (bf16[1,64,512]{2,1,0:T(8,128)(2,1)}, bf16[2,5,192,128]{3,2,1,0:T(8,128)(2,1)S(1)}, bf16[8,80,128]{2,1,0:T(8,128)(2,1)S(1)}, bf16[2,240,64]{2,1,0:T(8,128)(2,1)S(1)}) custom-call(s32[1]{0:T(128)} %bitcast.even_ref, bf16[1,64,512]{2,1,0:T(8,128)(2,1)S(1)} %bitcast.42, bf16[1,64,512]{2,1,0:T(8,128)(2,1)S(1)} %bitcast.44, ...), custom_call_target="tpu_custom_call" | custom-call | flops 10000000000 | bytes 4194304 | tf_op jit(solution)/shard_map/pallas_call | solution.py:354
  15.8 0.1 collective-permute-start.2
  16.0 1.5 %collective-permute-done.2 = bf16[4,240,128]{2,1,0:T(8,128)(2,1)S(1)} collective-permute-done((bf16[4,240,128]{2,1,0:T(8,128)(2,1)S(1)}, bf16[4,240,128]{2,1,0:T(8,128)(2,1)S(1)}, u32[]{:S(2)}, u32[]{:S(2)}) %collective-permute-start.2) | collective-permute-done | bytes 245792 | tf_op jit(solution)/shard_map/ppermute | solution.py:426
  17.4 0.1 fusion
  17.5 4.4 %collective-permute-start.3 = (bf16[240,128]{1,0:T(8,128)(2,1)S(1)}, bf16[240,128]{1,0:T(8,128)(2,1)S(1)}, u32[]{:S(2)}, u32[]{:S(2)}) collective-permute-start(bf16[240,128]{1,0:T(8,128)(2,1)S(1)} %get-tuple-element.32), channel_id=1, source_target_pairs={{0,1},{1,0},{2,3},{3,2},{4,5},{5,4},{6,7},{7,6},{8,9},{9,8},{10,11... | collective-permute-start | bytes 184328 | tf_op jit(solution)/shard_map/ppermute | solution.py:426
  21.9 1.5 %collective-permute-start.4 = (bf16[240,128]{1,0:T(8,128)(2,1)S(1)}, bf16[240,128]{1,0:T(8,128)(2,1)S(1)}, u32[]{:S(2)}, u32[]{:S(2)}) collective-permute-start(bf16[240,128]{1,0:T(8,128)(2,1)S(1)} %get-tuple-element.34), channel_id=1, source_target_pairs={{0,16},{1,17},{2,18},{3,19},{4,20},{5,21},{6,22},{7,23},{8,24},{9,... | collective-permute-start | bytes 184328 | tf_op jit(solution)/shard_map/ppermute | solution.py:426
  23.4 0.1 collective-permute-start.5
  23.4 0.8 %collective-permute-done.3 = bf16[240,128]{1,0:T(8,128)(2,1)S(1)} collective-permute-done((bf16[240,128]{1,0:T(8,128)(2,1)S(1)}, bf16[240,128]{1,0:T(8,128)(2,1)S(1)}, u32[]{:S(2)}, u32[]{:S(2)}) %collective-permute-start.3) | collective-permute-done | bytes 61472 | tf_op jit(solution)/shard_map/ppermute | solution.py:426
  24.2 2.5 %collective-permute-done.4 = bf16[240,128]{1,0:T(8,128)(2,1)S(1)} collective-permute-done((bf16[240,128]{1,0:T(8,128)(2,1)S(1)}, bf16[240,128]{1,0:T(8,128)(2,1)S(1)}, u32[]{:S(2)}, u32[]{:S(2)}) %collective-permute-start.4) | collective-permute-done | bytes 61472 | tf_op jit(solution)/shard_map/ppermute | solution.py:426
  26.7 1.8 %collective-permute-done.5 = bf16[240,128]{1,0:T(8,128)(2,1)S(1)} collective-permute-done((bf16[240,128]{1,0:T(8,128)(2,1)S(1)}, bf16[240,128]{1,0:T(8,128)(2,1)S(1)}, u32[]{:S(2)}, u32[]{:S(2)}) %collective-permute-start.5) | collective-permute-done | bytes 61472 | tf_op jit(solution)/shard_map/ppermute | solution.py:426
  28.5 1.6 %collective-permute-start.6 = (bf16[240,128]{1,0:T(8,128)(2,1)S(1)}, bf16[240,128]{1,0:T(8,128)(2,1)S(1)}, u32[]{:S(2)}, u32[]{:S(2)}) collective-permute-start(bf16[240,128]{1,0:T(8,128)(2,1)S(1)} %fusion.2), channel_id=1, source_target_pairs={{0,2},{1,3},{2,0},{3,1},{4,6},{5,7},{6,4},{7,5},{8,10},{9,11},{10,... | collective-permute-start | bytes 184328 | tf_op jit(solution)/shard_map/ppermute | solution.py:426
  30.2 2.1 %collective-permute-start.7 = (bf16[240,128]{1,0:T(8,128)(2,1)S(1)}, bf16[240,128]{1,0:T(8,128)(2,1)S(1)}, u32[]{:S(2)}, u32[]{:S(2)}) collective-permute-start(bf16[240,128]{1,0:T(8,128)(2,1)S(1)} %fusion.2), channel_id=1, source_target_pairs={{0,4},{1,5},{2,6},{3,7},{4,0},{5,1},{6,2},{7,3},{8,12},{9,13},{10,... | collective-permute-start | bytes 184328 | tf_op jit(solution)/shard_map/ppermute | solution.py:426
  32.2 0.7 %collective-permute-start.8 = (bf16[240,128]{1,0:T(8,128)(2,1)S(1)}, bf16[240,128]{1,0:T(8,128)(2,1)S(1)}, u32[]{:S(2)}, u32[]{:S(2)}) collective-permute-start(bf16[240,128]{1,0:T(8,128)(2,1)S(1)} %fusion.2), channel_id=1, source_target_pairs={{0,6},{1,7},{2,4},{3,5},{4,2},{5,3},{6,0},{7,1},{8,14},{9,15},{10,... | collective-permute-start | bytes 184328 | tf_op jit(solution)/shard_map/ppermute | solution.py:426
  33.0 0.4 collective-permute-done.6
  33.4 3.2 %collective-permute-done.7 = bf16[240,128]{1,0:T(8,128)(2,1)S(1)} collective-permute-done((bf16[240,128]{1,0:T(8,128)(2,1)S(1)}, bf16[240,128]{1,0:T(8,128)(2,1)S(1)}, u32[]{:S(2)}, u32[]{:S(2)}) %collective-permute-start.7) | collective-permute-done | bytes 61472 | tf_op jit(solution)/shard_map/ppermute | solution.py:426
  36.6 1.7 %collective-permute-done.8 = bf16[240,128]{1,0:T(8,128)(2,1)S(1)} collective-permute-done((bf16[240,128]{1,0:T(8,128)(2,1)S(1)}, bf16[240,128]{1,0:T(8,128)(2,1)S(1)}, u32[]{:S(2)}, u32[]{:S(2)}) %collective-permute-start.8) | collective-permute-done | bytes 61472 | tf_op jit(solution)/shard_map/ppermute | solution.py:426
  38.3 0.1 bitcast_dynamic-update-slice_fusion.3
  38.4 1.8 %collective-permute-start.9 = (bf16[240,128]{1,0:T(8,128)(2,1)S(1)}, bf16[240,128]{1,0:T(8,128)(2,1)S(1)}, u32[]{:S(2)}, u32[]{:S(2)}) collective-permute-start(bf16[240,128]{1,0:T(8,128)(2,1)S(1)} %get-tuple-element.31), channel_id=1, source_target_pairs={{0,1},{1,0},{2,3},{3,2},{4,5},{5,4},{6,7},{7,6},{8,9},{9,8},{10,11... | collective-permute-start | bytes 184328 | tf_op jit(solution)/shard_map/ppermute | solution.py:426
  40.2 0.5 %collective-permute-start.10 = (bf16[240,128]{1,0:T(8,128)(2,1)S(1)}, bf16[240,128]{1,0:T(8,128)(2,1)S(1)}, u32[]{:S(2)}, u32[]{:S(2)}) collective-permute-start(bf16[240,128]{1,0:T(8,128)(2,1)S(1)} %get-tuple-element.31), channel_id=1, source_target_pairs={{0,16},{1,17},{2,18},{3,19},{4,20},{5,21},{6,22},{7,23},{8,24},{9,... | collective-permute-start | bytes 184328 | tf_op jit(solution)/shard_map/ppermute | solution.py:426
  40.7 1.2 %collective-permute-start.11 = (bf16[240,128]{1,0:T(8,128)(2,1)S(1)}, bf16[240,128]{1,0:T(8,128)(2,1)S(1)}, u32[]{:S(2)}, u32[]{:S(2)}) collective-permute-start(bf16[240,128]{1,0:T(8,128)(2,1)S(1)} %get-tuple-element.31), channel_id=1, source_target_pairs={{0,17},{1,16},{2,19},{3,18},{4,21},{5,20},{6,23},{7,22},{8,25},{9,... | collective-permute-start | bytes 184328 | tf_op jit(solution)/shard_map/ppermute | solution.py:426
  41.9 0.7 %collective-permute-done.9 = bf16[240,128]{1,0:T(8,128)(2,1)S(1)} collective-permute-done((bf16[240,128]{1,0:T(8,128)(2,1)S(1)}, bf16[240,128]{1,0:T(8,128)(2,1)S(1)}, u32[]{:S(2)}, u32[]{:S(2)}) %collective-permute-start.9) | collective-permute-done | bytes 61472 | tf_op jit(solution)/shard_map/ppermute | solution.py:426
  42.7 1.7 %collective-permute-done.10 = bf16[240,128]{1,0:T(8,128)(2,1)S(1)} collective-permute-done((bf16[240,128]{1,0:T(8,128)(2,1)S(1)}, bf16[240,128]{1,0:T(8,128)(2,1)S(1)}, u32[]{:S(2)}, u32[]{:S(2)}) %collective-permute-start.10) | collective-permute-done | bytes 61472 | tf_op jit(solution)/shard_map/ppermute | solution.py:426
  44.4 1.4 %collective-permute-done.11 = bf16[240,128]{1,0:T(8,128)(2,1)S(1)} collective-permute-done((bf16[240,128]{1,0:T(8,128)(2,1)S(1)}, bf16[240,128]{1,0:T(8,128)(2,1)S(1)}, u32[]{:S(2)}, u32[]{:S(2)}) %collective-permute-start.11) | collective-permute-done | bytes 61472 | tf_op jit(solution)/shard_map/ppermute | solution.py:426
  45.8 0.1 collective-permute-start.12
  45.9 1.4 %shard_map.96 = bf16[1,64,512]{2,1,0:T(8,128)(2,1)} custom-call(bf16[8,80,128]{2,1,0:T(8,128)(2,1)S(1)} %get-tuple-element.24.delta_ref, bf16[2,240,64]{2,1,0:T(8,128)(2,1)S(1)} %get-tuple-element.25.pick_ref, bf16[640,256]{1,0:T(8,128)(2,1)S(1)} %get-tuple-element.26.b1_ref), custom_call_target="tpu_custom_call" | custom-call | flops 1000000000 | bytes 2097152 | tf_op jit(solution)/shard_map/pallas_call | solution.py:383
  47.3 0.1 collective-permute-done.12
  47.4 1.1 %shard_map.97 = (f32[64,1728]{1,0:T(8,128)}, f32[64,1728]{1,0:T(8,128)}) custom-call(s32[1]{0:T(128)} %bitcast.7.refs_0_, bf16[5,192,128]{2,1,0:T(8,128)(2,1)S(1)} %bitcast.35, bf16[5,192,128]{2,1,0:T(8,128)(2,1)S(1)} %bitcast.38), custom_call_target="tpu_custom_call" | custom-call | tf_op jit(solution)/shard_map/pallas_call | solution.py:411
  (7 shorter events, 0.2 us)
Async XLA Ops:
  0.6 0.7 %copy-start.6 = (s32[1,1000]{1,0:T(1,128)S(1)}, s32[1,1000]{1,0:T(1,128)}, u32[]{:S(2)}) copy-start(s32[1,1000]{1,0:T(1,128)} %gather_ref.1) | copy-start | bytes 12004
  0.6 0.7 %copy-start.7 = (s32[1,128]{1,0:T(1,128)S(1)}, s32[1,128]{1,0:T(1,128)}, u32[]{:S(2)}) copy-start(s32[1,128]{1,0:T(1,128)} %send_ref.1) | copy-start | bytes 1540
  1.3 0.8 %copy-start.2 = (bf16[1,512,64]{1,2,0:T(8,128)(2,1)S(1)}, bf16[1,512,64]{1,2,0:T(8,128)(2,1)}, u32[]{:S(2)}) copy-start(bf16[1,512,64]{1,2,0:T(8,128)(2,1)} %param.6) | copy-start | bytes 196612
  2.2 0.8 %copy-start.4 = (bf16[1,512,64]{1,2,0:T(8,128)(2,1)S(1)}, bf16[1,512,64]{1,2,0:T(8,128)(2,1)}, u32[]{:S(2)}) copy-start(bf16[1,512,64]{1,2,0:T(8,128)(2,1)} %param.7) | copy-start | bytes 196612
  3.2 5.8 %collective-permute-start = (bf16[200,128]{1,0:T(8,128)(2,1)S(1)}, bf16[200,128]{1,0:T(8,128)(2,1)S(1)}, u32[]{:S(2)}, u32[]{:S(2)}) collective-permute-start(bf16[200,128]{1,0:T(8,128)(2,1)S(1)} %get-tuple-element.17), channel_id=1, source_target_pairs={{0,1},{1,0},{2,3},{3,2},{4,5},{5,4},{6,7},{7,6},{8,9},{9,8},{10,11... | collective-permute-start | bytes 153608 | tf_op jit(solution)/shard_map/ppermute | solution.py:469
  6.3 2.8 %collective-permute-start.1 = (bf16[200,128]{1,0:T(8,128)(2,1)S(1)}, bf16[200,128]{1,0:T(8,128)(2,1)S(1)}, u32[]{:S(2)}, u32[]{:S(2)}) collective-permute-start(bf16[200,128]{1,0:T(8,128)(2,1)S(1)} %get-tuple-element.18), channel_id=1, source_target_pairs={{1,2},{2,1},{3,4},{4,3},{5,6},{6,5},{9,10},{10,9},{11,12},{12,11},... | collective-permute-start | bytes 153608 | tf_op jit(solution)/shard_map/ppermute | solution.py:470
  7.0 0.9 %copy-start = (bf16[1728,64]{0,1:T(8,128)(2,1)S(1)}, bf16[1728,64]{0,1:T(8,128)(2,1)}, u32[]{:S(2)}) copy-start(bf16[1728,64]{0,1:T(8,128)(2,1)} %param.8) | copy-start | bytes 663556
  7.9 0.9 %copy-start.1 = (bf16[1728,64]{0,1:T(8,128)(2,1)S(1)}, bf16[1728,64]{0,1:T(8,128)(2,1)}, u32[]{:S(2)}) copy-start(bf16[1728,64]{0,1:T(8,128)(2,1)} %param.9) | copy-start | bytes 663556
  8.8 0.8 %copy-start.3 = (bf16[1,512,64]{1,2,0:T(8,128)(2,1)S(1)}, bf16[1,512,64]{1,2,0:T(8,128)(2,1)}, u32[]{:S(2)}) copy-start(bf16[1,512,64]{1,2,0:T(8,128)(2,1)} %param.6) | copy-start | bytes 196612
  8.8 0.9 %copy-start.5 = (bf16[1,512,64]{1,2,0:T(8,128)(2,1)S(1)}, bf16[1,512,64]{1,2,0:T(8,128)(2,1)}, u32[]{:S(2)}) copy-start(bf16[1,512,64]{1,2,0:T(8,128)(2,1)} %param.7) | copy-start | bytes 196612
  15.8 1.6 %collective-permute-start.2 = (bf16[4,240,128]{2,1,0:T(8,128)(2,1)S(1)}, bf16[4,240,128]{2,1,0:T(8,128)(2,1)S(1)}, u32[]{:S(2)}, u32[]{:S(2)}) collective-permute-start(bf16[4,240,128]{2,1,0:T(8,128)(2,1)S(1)} %dynamic-slice_bitcast_fusion), channel_id=1, source_target_pairs={{0,8},{1,9},{2,10},{3,11},{4,12},{5,13},{6,14},{7,15},{8,0},{9,1},... | collective-permute-start | bytes 737288 | tf_op jit(solution)/shard_map/ppermute | solution.py:426
  17.5 6.7 %collective-permute-start.3 = (bf16[240,128]{1,0:T(8,128)(2,1)S(1)}, bf16[240,128]{1,0:T(8,128)(2,1)S(1)}, u32[]{:S(2)}, u32[]{:S(2)}) collective-permute-start(bf16[240,128]{1,0:T(8,128)(2,1)S(1)} %get-tuple-element.32), channel_id=1, source_target_pairs={{0,1},{1,0},{2,3},{3,2},{4,5},{5,4},{6,7},{7,6},{8,9},{9,8},{10,11... | collective-permute-start | bytes 184328 | tf_op jit(solution)/shard_map/ppermute | solution.py:426
  21.9 4.8 %collective-permute-start.4 = (bf16[240,128]{1,0:T(8,128)(2,1)S(1)}, bf16[240,128]{1,0:T(8,128)(2,1)S(1)}, u32[]{:S(2)}, u32[]{:S(2)}) collective-permute-start(bf16[240,128]{1,0:T(8,128)(2,1)S(1)} %get-tuple-element.34), channel_id=1, source_target_pairs={{0,16},{1,17},{2,18},{3,19},{4,20},{5,21},{6,22},{7,23},{8,24},{9,... | collective-permute-start | bytes 184328 | tf_op jit(solution)/shard_map/ppermute | solution.py:426
  23.4 5.1 %collective-permute-start.5 = (bf16[240,128]{1,0:T(8,128)(2,1)S(1)}, bf16[240,128]{1,0:T(8,128)(2,1)S(1)}, u32[]{:S(2)}, u32[]{:S(2)}) collective-permute-start(bf16[240,128]{1,0:T(8,128)(2,1)S(1)} %get-tuple-element.33), channel_id=1, source_target_pairs={{0,17},{1,16},{2,19},{3,18},{4,21},{5,20},{6,23},{7,22},{8,25},{9,... | collective-permute-start | bytes 184328 | tf_op jit(solution)/shard_map/ppermute | solution.py:426
  28.5 4.9 %collective-permute-start.6 = (bf16[240,128]{1,0:T(8,128)(2,1)S(1)}, bf16[240,128]{1,0:T(8,128)(2,1)S(1)}, u32[]{:S(2)}, u32[]{:S(2)}) collective-permute-start(bf16[240,128]{1,0:T(8,128)(2,1)S(1)} %fusion.2), channel_id=1, source_target_pairs={{0,2},{1,3},{2,0},{3,1},{4,6},{5,7},{6,4},{7,5},{8,10},{9,11},{10,... | collective-permute-start | bytes 184328 | tf_op jit(solution)/shard_map/ppermute | solution.py:426
  30.2 6.4 %collective-permute-start.7 = (bf16[240,128]{1,0:T(8,128)(2,1)S(1)}, bf16[240,128]{1,0:T(8,128)(2,1)S(1)}, u32[]{:S(2)}, u32[]{:S(2)}) collective-permute-start(bf16[240,128]{1,0:T(8,128)(2,1)S(1)} %fusion.2), channel_id=1, source_target_pairs={{0,4},{1,5},{2,6},{3,7},{4,0},{5,1},{6,2},{7,3},{8,12},{9,13},{10,... | collective-permute-start | bytes 184328 | tf_op jit(solution)/shard_map/ppermute | solution.py:426
  32.2 6.0 %collective-permute-start.8 = (bf16[240,128]{1,0:T(8,128)(2,1)S(1)}, bf16[240,128]{1,0:T(8,128)(2,1)S(1)}, u32[]{:S(2)}, u32[]{:S(2)}) collective-permute-start(bf16[240,128]{1,0:T(8,128)(2,1)S(1)} %fusion.2), channel_id=1, source_target_pairs={{0,6},{1,7},{2,4},{3,5},{4,2},{5,3},{6,0},{7,1},{8,14},{9,15},{10,... | collective-permute-start | bytes 184328 | tf_op jit(solution)/shard_map/ppermute | solution.py:426
  38.4 4.3 %collective-permute-start.9 = (bf16[240,128]{1,0:T(8,128)(2,1)S(1)}, bf16[240,128]{1,0:T(8,128)(2,1)S(1)}, u32[]{:S(2)}, u32[]{:S(2)}) collective-permute-start(bf16[240,128]{1,0:T(8,128)(2,1)S(1)} %get-tuple-element.31), channel_id=1, source_target_pairs={{0,1},{1,0},{2,3},{3,2},{4,5},{5,4},{6,7},{7,6},{8,9},{9,8},{10,11... | collective-permute-start | bytes 184328 | tf_op jit(solution)/shard_map/ppermute | solution.py:426
  40.2 4.2 %collective-permute-start.10 = (bf16[240,128]{1,0:T(8,128)(2,1)S(1)}, bf16[240,128]{1,0:T(8,128)(2,1)S(1)}, u32[]{:S(2)}, u32[]{:S(2)}) collective-permute-start(bf16[240,128]{1,0:T(8,128)(2,1)S(1)} %get-tuple-element.31), channel_id=1, source_target_pairs={{0,16},{1,17},{2,18},{3,19},{4,20},{5,21},{6,22},{7,23},{8,24},{9,... | collective-permute-start | bytes 184328 | tf_op jit(solution)/shard_map/ppermute | solution.py:426
  40.7 5.1 %collective-permute-start.11 = (bf16[240,128]{1,0:T(8,128)(2,1)S(1)}, bf16[240,128]{1,0:T(8,128)(2,1)S(1)}, u32[]{:S(2)}, u32[]{:S(2)}) collective-permute-start(bf16[240,128]{1,0:T(8,128)(2,1)S(1)} %get-tuple-element.31), channel_id=1, source_target_pairs={{0,17},{1,16},{2,19},{3,18},{4,21},{5,20},{6,23},{7,22},{8,25},{9,... | collective-permute-start | bytes 184328 | tf_op jit(solution)/shard_map/ppermute | solution.py:426
  45.8 1.6 %collective-permute-start.12 = (bf16[4,240,128]{2,1,0:T(8,128)(2,1)S(1)}, bf16[4,240,128]{2,1,0:T(8,128)(2,1)S(1)}, u32[]{:S(2)}, u32[]{:S(2)}) collective-permute-start(bf16[4,240,128]{2,1,0:T(8,128)(2,1)S(1)} %bitcast_dynamic-update-slice_fusion), channel_id=1, source_target_pairs={{0,8},{1,9},{2,10},{3,11},{4,12},{5,13},{6,14},{7,15},{8,0},{9,1},... | collective-permute-start | bytes 737288 | tf_op jit(solution)/shard_map/ppermute | solution.py:426
where the time goes:
time: 48.9 us; the launch traced here: 48.5 us
  starting transfers between devices  17.8 us (36%)
  waiting for transfers between devices  15.8 us (32%)
  Pallas kernels  9.02 us (18%)
  local copies, waits for them, and re-layouts  4.99 us (10%)
  between operations  0.78 us (2%)
    ppermute x11, waiting for transfers between devices, xor_permute(): return lax.ppermute(v, BOTH, pairs)  15.8 us
    ppermute x11, starting transfers between devices, xor_permute(): return lax.ppermute(v, BOTH, pairs)  14 us
    pallas_call x1, Pallas kernels, main_call(): pl.pallas_call(main_kernel, out_shape=(jax.ShapeDtypeStruct(feat.shape, B...  6.12 us
    unnamed x16, local copies, waits for them, and re-layouts  4.88 us
    ppermute x1, starting transfers between devices, step(): first = lax.ppermute(first, 'brick', within)  3.08 us
    pallas_call x1, Pallas kernels, last_call(): pl.pallas_call(last_kernel, out_shape=jax.ShapeDtypeStruct(shape, BF16),...  1.39 us
    pallas_call x1, Pallas kernels, finish(): pl.pallas_call(lambda *refs: finish_kernel(scale, *refs), out_shape=(shap...  1.12 us
  transfers between devices with their start and end apart: 13, of which 11 were waited for; matrix products, arithmetic and copies ran while one was open for 0% of the time, Pallas kernels for 3%

commit v1 on v0

--- a/solution.py
+++ b/solution.py
@@ -27,10 +27,12 @@
 KDIM = TILES * 2 * C
 LOW, OWN, HIGH = 0, 6, 16
 PLANES = 20
+SPLIT = 4
 WIDE = 4
 SPAN = 2
 
 LIMIT = pltpu.CompilerParams(vmem_limit_bytes=24 << 20)
+HBM_SPEC = pl.BlockSpec(memory_space=pltpu.HBM)
 VMEM_SPEC = pl.BlockSpec(memory_space=pltpu.VMEM)
 SMEM_SPEC = pl.BlockSpec(memory_space=pltpu.SMEM)
 
@@ -48,7 +50,8 @@
     return lax.broadcasted_iota(jnp.int32, shape, len(shape) - 1) % (2 * C) < C
 
 
-def weight_kernel(w1_ref, w2_ref, f1_ref, f2_ref, b1_ref, b2_ref):
+def weight_kernel(w1_hbm, w2_hbm, f1_ref, f2_ref, b1_ref, b2_ref, w1_ref, w2_ref, sems):
+    fetch(((w1_hbm, w1_ref), (w2_hbm, w2_ref)), sems)
     zero = jnp.zeros((C, C), BF16)
     for w_ref, f_ref, b_ref in ((w1_ref, f1_ref, b1_ref), (w2_ref, f2_ref, b2_ref)):
         blocks = [w_ref[:, o * C : (o + 1) * C] for o in range(27)]
@@ -72,11 +75,12 @@
     return pl.pallas_call(
         weight_kernel,
         out_shape=(fwd, fwd, bwd, bwd),
-        in_specs=[VMEM_SPEC] * 2,
+        in_specs=[HBM_SPEC] * 2,
         out_specs=(VMEM_SPEC,) * 4,
+        scratch_shapes=[pltpu.VMEM(w1.shape, BF16)] * 2 + [pltpu.SemaphoreType.DMA((2,))],
         compiler_params=LIMIT,
         cost_estimate=pl.CostEstimate(flops=0, bytes_accessed=2 << 20, transcendentals=0),
-    )(w1, w2)
+    )(*(pltpu.with_memory_space_constraint(v, pltpu.HBM) for v in (w1, w2)))
 
 
 def rim_spread(first):
@@ -87,7 +91,38 @@
     return jnp.where(lax.broadcasted_iota(jnp.int32, (2 * C, 4 * C), 0) == source, 1.0, 0.0).astype(BF16)
 
 
-def pack_kernel(even_ref, feat_ref, cot_ref, send_ref, gather_ref, first_ref, second_ref, codes_ref):
+def fetch(pairs, sems):
+    copies = [pltpu.make_async_copy(a, b, sems.at[k]) for k, (a, b) in enumerate(pairs)]
+    for copy in copies:
+        copy.start()
+    for copy in copies:
+        copy.wait()
+
+
+def pack_kernel(
+    even_ref,
+    feat_hbm,
+    cot_hbm,
+    send_hbm,
+    gather_hbm,
+    first_ref,
+    second_ref,
+    codes_ref,
+    feat_ref,
+    cot_ref,
+    send_ref,
+    gather_ref,
+    sems,
+):
+    fetch(
+        (
+            (feat_hbm, feat_ref),
+            (cot_hbm, cot_ref),
+            (send_hbm, send_ref),
+            (gather_hbm, gather_ref),
+        ),
+        sems,
+    )
     send = send_ref[...]
     upper = lax.broadcasted_iota(jnp.int32, send.shape, 1) >= FACE
     row = jnp.where(upper, send - (VOX - FACE), send)
@@ -132,11 +167,17 @@
     return pl.pallas_call(
         pack_kernel,
         out_shape=(jax.ShapeDtypeStruct((rows, 2 * C), BF16),) * 2
-        + (jax.ShapeDtypeStruct((E, 2 * C), BF16),),
-        in_specs=[SMEM_SPEC] + [VMEM_SPEC] * 4,
-        out_specs=(VMEM_SPEC,) * 3,
+        + (jax.ShapeDtypeStruct((E, 2 * C), BF16),)
+        + (jax.ShapeDtypeStruct(feat.shape, BF16),) * 2,
+        in_specs=[SMEM_SPEC] + [HBM_SPEC] * 4,
+        out_specs=(VMEM_SPEC,) * 5,
+        scratch_shapes=[
+            pltpu.VMEM(send.shape, jnp.int32),
+            pltpu.VMEM(gather.shape, jnp.int32),
+            pltpu.SemaphoreType.DMA((4,)),
+        ],
         compiler_params=LIMIT,
-    )(even, feat, cot, send, gather)
+    )(even, *(pltpu.with_memory_space_constraint(v, pltpu.HBM) for v in (feat, cot, send, gather)))
 
 
 def z_shifted(v):
@@ -284,11 +325,15 @@
     pick_ref[0] = picks[1]
     pick_ref[1] = picks[2]
 
-    def conv(q_ref, w, flipped=False):
-        q = q_ref[...].reshape(E * PLANES * E, KDIM)
+    def conv(q_ref, w, flipped=False, skip=0):
         dims = (((1,), (0 if flipped else 1,)), ((), ()))
-        r = lax.dot_general(q, w, dims, preferred_element_type=F32)
-        return r.reshape(E, PLANES, E, 4 * C)
+        step = E // SPLIT
+        parts = []
+        for y in range(0, E, step):
+            q = q_ref[y : y + step, skip * E : (PLANES - skip) * E, :].reshape(-1, KDIM)
+            r = lax.dot_general(q, w, dims, preferred_element_type=F32)
+            parts.append(r.reshape(step, PLANES - 2 * skip, E, 4 * C))
+        return jnp.concatenate(parts, axis=0)
 
     def rounded(v):
         return v.astype(BF16).astype(F32)
@@ -325,7 +370,8 @@
     )
     r = conv(q2_ref, f2_ref[...])
     second_own = x_taps(r, OWN, E)
-    put_rows(out_ref, second_own * sigmoid(second_own))
+    out = second_own * sigmoid(second_own)
+    out_ref[...] = out.reshape(E, FACE, 2 * C).astype(BF16)
     second_low = x_taps(r, LOW + WIDE - SPAN, SPAN)
     second_high = x_taps(r, HIGH, SPAN)
     delta_own = rounded(own_c * slope(second_own))
@@ -340,10 +386,11 @@
         jnp.concatenate([delta_high, pads], axis=1),
         picks,
     )
-    r = conv(q3_ref, b2_ref[...], True)
-    first_own = rounded(x_taps(r, OWN, E) * slope(pre_own))
-    first_low = rounded(x_taps(r, LOW + WIDE - 1, 1) * slope(pre_low[:, -1:]))
-    first_high = rounded(x_taps(r, HIGH, 1) * slope(pre_high[:, :1]))
+    skip = WIDE - SPAN
+    r = conv(q3_ref, b2_ref[...], True, skip)
+    first_own = rounded(x_taps(r, OWN - skip, E) * slope(pre_own))
+    first_low = rounded(x_taps(r, LOW + WIDE - 1 - skip, 1) * slope(pre_low[:, -1:]))
+    first_high = rounded(x_taps(r, HIGH - skip, 1) * slope(pre_high[:, :1]))
     weight_gradient(0, q1_ref, first_own)
     delta = jnp.concatenate([first_low, first_own, first_high], axis=1)
     delta_ref[...] = delta.reshape(E, (E + 2) * E, 2 * C).astype(BF16)
@@ -354,7 +401,7 @@
     return pl.pallas_call(
         main_kernel,
         out_shape=(
-            jax.ShapeDtypeStruct(feat.shape, BF16),
+            jax.ShapeDtypeStruct((E, FACE, 2 * C), BF16),
             jax.ShapeDtypeStruct((2, TILES, 3 * C, 2 * C), BF16),
             jax.ShapeDtypeStruct((E, (E + 2) * E, 2 * C), BF16),
             jax.ShapeDtypeStruct((2, CELLS, FACE), BF16),
@@ -367,7 +414,8 @@
     )(even, feat, cot, first, second, codes, f1, f2, b2)
 
 
-def last_kernel(delta_ref, pick_ref, b1_ref, out_ref, q_ref):
+def last_kernel(rows_ref, delta_ref, pick_ref, b1_ref, out_ref, grad_ref, q_ref):
+    put_rows(out_ref, rows_ref[...].astype(F32).reshape(E, E, E, 2 * C))
     delta = delta_ref[...].astype(F32).reshape(E, E + 2, E, 2 * C)
     put_interior(q_ref, 2, delta[:, 1 : E + 1])
     below = rim_cells(pick_ref[0], delta[:, 0])
@@ -376,19 +424,19 @@
     put_rims(q_ref, E + 2, [above, above])
     q = q_ref[...].reshape(E * (E + 4) * E, KDIM)
     r = jnp.dot(q, b1_ref[...], preferred_element_type=F32)
-    put_rows(out_ref, x_taps(r.reshape(E, E + 4, E, 4 * C), 2, E))
-
-
-def last_call(delta, pick, b1, shape):
+    put_rows(grad_ref, x_taps(r.reshape(E, E + 4, E, 4 * C), 2, E))
+
+
+def last_call(rows, delta, pick, b1, shape):
     return pl.pallas_call(
         last_kernel,
-        out_shape=jax.ShapeDtypeStruct(shape, BF16),
-        in_specs=[VMEM_SPEC] * 3,
-        out_specs=VMEM_SPEC,
+        out_shape=(jax.ShapeDtypeStruct(shape, BF16),) * 2,
+        in_specs=[VMEM_SPEC] * 4,
+        out_specs=(VMEM_SPEC,) * 2,
         scratch_shapes=[pltpu.VMEM((E, (E + 4) * E, KDIM), BF16)],
         compiler_params=LIMIT,
         cost_estimate=pl.CostEstimate(flops=10**9, bytes_accessed=2 << 20, transcendentals=0),
-    )(delta, pick, b1)
+    )(rows, delta, pick, b1)
 
 
 def finish_kernel(scale, flag_ref, mine_ref, theirs_ref, g1_ref, g2_ref):
@@ -426,6 +474,13 @@
     return lax.ppermute(v, BOTH, pairs)
 
 
+def exchange(pieces):
+    out = []
+    for k, piece in zip((1, 2, 3), pieces):
+        out.append(xor_permute(piece, 2 * (k >> 1), k & 1))
+    return out
+
+
 def all_sum(v):
     scenes, bricks = lax.axis_size("scene"), lax.axis_size("brick")
     if scenes != 4 or bricks != 8:
@@ -444,13 +499,13 @@
 
     other = xor_permute(pick(parts, 1 - core), 1, 0)
     chip = (pick(parts, core).astype(F32) + other.astype(F32)).astype(BF16)
-    moved = [
-        xor_permute(pick(chip, where ^ k), 2 * (k >> 1), k & 1) for k in (1, 2, 3)
-    ]
+    moved = exchange([pick(chip, where ^ k) for k in (1, 2, 3)])
     plane = sum4(pick(chip, where), *moved).astype(BF16)
-    column = [xor_permute(plane, 0, 2 * k) for k in (1, 2, 3)]
-    whole = sum4(plane, *column).astype(BF16)
-    back = [xor_permute(whole, 2 * (k >> 1), k & 1) for k in (1, 2, 3)]
+    other = xor_permute(plane, 0, 2)
+    pair = (plane.astype(F32) + other.astype(F32)).astype(BF16)
+    other = xor_permute(pair, 0, 4)
+    whole = (pair.astype(F32) + other.astype(F32)).astype(BF16)
+    back = exchange([whole] * 3)
     mine = jnp.zeros(chip.shape, BF16)
     for k, piece in enumerate([whole] + back):
         mine = lax.dynamic_update_index_in_dim(mine, piece, where ^ k, 0)
@@ -463,15 +518,15 @@
     even = 1 - (lax.axis_index("brick") & 1)[None]
     feat, cot = jnp.swapaxes(features, 1, 2), jnp.swapaxes(cotangent, 1, 2)
 
-    first, second, codes = pack(even, feat, cot, send_rows, gather_rows)
+    first, second, codes, feat, cot = pack(even, feat, cot, send_rows, gather_rows)
     within = [(i, i ^ 1) for i in range(bricks) if i ^ 1 < bricks]
     between = [(i, ((i + 1) ^ 1) - 1) for i in range(1, bricks) if ((i + 1) ^ 1) - 1 < bricks]
     first = lax.ppermute(first, "brick", within)
     second = lax.ppermute(second, "brick", between)
     f1, f2, b1, b2 = prepare_weights(first_weight.T, second_weight.T)
 
-    output, grads, delta, pick = main_call(even, feat, cot, first, second, codes, f1, f2, b2)
-    grad_input = last_call(delta, pick, b1, feat.shape)
+    rows, grads, delta, pick = main_call(even, feat, cot, first, second, codes, f1, f2, b2)
+    output, grad_input = last_call(rows, delta, pick, b1, feat.shape)
     flag, mine, theirs = all_sum(grads)
     scale = float(lax.axis_size("scene") * bricks * VOX) ** -0.5
     grad_first, grad_second = finish(flag, mine, theirs, scale)

time: 48.9 us -> 43.8 us (0.90)
  local copies, waits for them, and re-layouts: 4.99 us -> 0.12 us
  starting transfers between devices: 17.8 us -> 18.6 us
    unnamed x16 -> x0, local copies, waits for them, and re-layouts: 4.88 us -> none
    pallas_call x3, Pallas kernels: 7.71 us -> 6.36 us  [the longest x1 3.71 us: main_call(): pl.pallas_call(main_kernel, out_shape=(jax.ShapeDtypeStruct((E, FACE, 2 *...]
    pallas_call x1, Pallas kernels: 0.19 us -> 1.11 us  [pack(): pl.pallas_call(pack_kernel, out_shape=(jax.ShapeDtypeStruct((rows, 2 * C)...]
    ppermute x11 -> x10, starting transfers between devices: 14 us -> 14.8 us  [xor_permute(): return lax.ppermute(v, BOTH, pairs)]
    ppermute x11 -> x10, waiting for transfers between devices: 15.8 us -> 15.2 us  [xor_permute(): return lax.ppermute(v, BOTH, pairs)]
  transfers between devices with their start and end apart: 13 -> 12, of which waited for: 11 -> 11; matrix products, arithmetic and copies ran while one was open for 0% -> 0% of each run, Pallas kernels for 3% -> 6%
where the time goes in v1:
time: 43.8 us; the launch traced here: 43.6 us
  starting transfers between devices  18.6 us (42%)
  waiting for transfers between devices  15.4 us (35%)
  Pallas kernels  8.59 us (20%)
  between operations  0.76 us (2%)
    ppermute x10, waiting for transfers between devices, xor_permute(): return lax.ppermute(v, BOTH, pairs)  15.2 us
    ppermute x10, starting transfers between devices, xor_permute(): return lax.ppermute(v, BOTH, pairs)  14.8 us
    pallas_call x1, Pallas kernels, main_call(): pl.pallas_call(main_kernel, out_shape=(jax.ShapeDtypeStruct((E, FACE, 2 *...  3.71 us
    ppermute x1, starting transfers between devices, step(): first = lax.ppermute(first, 'brick', within)  3.08 us
    pallas_call x1, Pallas kernels, last_call(): pl.pallas_call(last_kernel, out_shape=(jax.ShapeDtypeStruct(shape, BF16),...  1.39 us
    pallas_call x1, Pallas kernels, prepare_weights(): pl.pallas_call(weight_kernel, out_shape=(fwd, fwd, bwd, bwd), in_specs=[H...  1.26 us
    pallas_call x1, Pallas kernels, finish(): pl.pallas_call(lambda *refs: finish_kernel(scale, *refs), out_shape=(shap...  1.12 us
    pallas_call x1, Pallas kernels, pack(): pl.pallas_call(pack_kernel, out_shape=(jax.ShapeDtypeStruct((rows, 2 * C)...  1.11 us
  transfers between devices with their start and end apart: 12, of which 11 were waited for; matrix products, arithmetic and copies ran while one was open for 0% of the time, Pallas kernels for 6%

profile of v1, /device:TPU:0, one launch (start us, length us, event | category | flops | bytes accessed | tf_op | source)
XLA Modules:
  0.0 43.6 jit_solution(3647236458450793179)
XLA Ops:
  0.6 1.1 %shard_map.93 = (bf16[200,128]{1,0:T(8,128)(2,1)S(1)}, bf16[200,128]{1,0:T(8,128)(2,1)S(1)}, bf16[8,128]{1,0:T(8,128)(2,1)S(1)}, bf16[1,64,512]{2,1,0:T(8,128)(2,1)S(1)}, bf16[1,64,512]{2,1,0:T(8,128)(2,1)S(1)}) custom-call(s32[1]{0:T(128)} %bitcast.even_ref, bf16[1,64,512]{2,1,0:T(8,128)(2,1)} %bitcast.41, bf16[1,64,512]{2,1,0:T(8,128)(2,1)} %bitcast.42, ...), custom_call_target="tpu_custom_call" | custom-call | tf_op jit(solution)/shard_map/pallas_call | solution.py:167
  1.8 3.1 %collective-permute-start = (bf16[200,128]{1,0:T(8,128)(2,1)S(1)}, bf16[200,128]{1,0:T(8,128)(2,1)S(1)}, u32[]{:S(2)}, u32[]{:S(2)}) collective-permute-start(bf16[200,128]{1,0:T(8,128)(2,1)S(1)} %get-tuple-element.23), channel_id=1, source_target_pairs={{0,1},{1,0},{2,3},{3,2},{4,5},{5,4},{6,7},{7,6},{8,9},{9,8},{10,11... | collective-permute-start | bytes 153608 | tf_op jit(solution)/shard_map/ppermute | solution.py:524
  4.8 0.7 %collective-permute-start.1 = (bf16[200,128]{1,0:T(8,128)(2,1)S(1)}, bf16[200,128]{1,0:T(8,128)(2,1)S(1)}, u32[]{:S(2)}, u32[]{:S(2)}) collective-permute-start(bf16[200,128]{1,0:T(8,128)(2,1)S(1)} %get-tuple-element.24), channel_id=1, source_target_pairs={{1,2},{2,1},{3,4},{4,3},{5,6},{6,5},{9,10},{10,9},{11,12},{12,11},... | collective-permute-start | bytes 153608 | tf_op jit(solution)/shard_map/ppermute | solution.py:525
  5.5 1.3 %shard_map.94 = (bf16[256,640]{1,0:T(8,128)(2,1)S(1)}, bf16[256,640]{1,0:T(8,128)(2,1)S(1)}, bf16[640,256]{1,0:T(8,128)(2,1)S(1)}, bf16[640,256]{1,0:T(8,128)(2,1)S(1)}) custom-call(bf16[64,1728]{1,0:T(8,128)(2,1)} %bitcast.39, bf16[64,1728]{1,0:T(8,128)(2,1)} %bitcast.40), custom_call_target="tpu_custom_call" | custom-call | bytes 2097152 | tf_op jit(solution)/shard_map/pallas_call | solution.py:75
  6.8 0.2 collective-permute-done.first_ref
  6.9 0.0 collective-permute-done.1.second_ref
  6.9 3.7 %shard_map.95 = (bf16[8,64,128]{2,1,0:T(8,128)(2,1)S(1)}, bf16[2,5,192,128]{3,2,1,0:T(8,128)(2,1)S(1)}, bf16[8,80,128]{2,1,0:T(8,128)(2,1)S(1)}, bf16[2,240,64]{2,1,0:T(8,128)(2,1)S(1)}) custom-call(s32[1]{0:T(128)} %bitcast.even_ref, bf16[1,64,512]{2,1,0:T(8,128)(2,1)S(1)} %get-tuple-element.21.feat_ref, bf16[1,64,512]{2,1,0:T(8,128)(2,1)S(1)} %get-tuple-element.22.cot_ref, ...), custom_call_target="tpu_custom_call" | custom-call | flops 10000000000 | bytes 4194304 | tf_op jit(solution)/shard_map/pallas_call | solution.py:401
  10.7 0.1 collective-permute-start.2
  10.8 1.5 %collective-permute-done.2 = bf16[4,240,128]{2,1,0:T(8,128)(2,1)S(1)} collective-permute-done((bf16[4,240,128]{2,1,0:T(8,128)(2,1)S(1)}, bf16[4,240,128]{2,1,0:T(8,128)(2,1)S(1)}, u32[]{:S(2)}, u32[]{:S(2)}) %collective-permute-start.2) | collective-permute-done | bytes 245792 | tf_op jit(solution)/shard_map/ppermute | solution.py:474
  12.2 0.1 fusion
  12.4 5.0 %collective-permute-start.3 = (bf16[240,128]{1,0:T(8,128)(2,1)S(1)}, bf16[240,128]{1,0:T(8,128)(2,1)S(1)}, u32[]{:S(2)}, u32[]{:S(2)}) collective-permute-start(bf16[240,128]{1,0:T(8,128)(2,1)S(1)} %get-tuple-element.40), channel_id=1, source_target_pairs={{0,1},{1,0},{2,3},{3,2},{4,5},{5,4},{6,7},{7,6},{8,9},{9,8},{10,11... | collective-permute-start | bytes 184328 | tf_op jit(solution)/shard_map/ppermute | solution.py:474
  17.3 1.9 %collective-permute-start.4 = (bf16[240,128]{1,0:T(8,128)(2,1)S(1)}, bf16[240,128]{1,0:T(8,128)(2,1)S(1)}, u32[]{:S(2)}, u32[]{:S(2)}) collective-permute-start(bf16[240,128]{1,0:T(8,128)(2,1)S(1)} %get-tuple-element.42), channel_id=1, source_target_pairs={{0,16},{1,17},{2,18},{3,19},{4,20},{5,21},{6,22},{7,23},{8,24},{9,... | collective-permute-start | bytes 184328 | tf_op jit(solution)/shard_map/ppermute | solution.py:474
  19.2 0.0 collective-permute-start.5
  19.2 0.5 %collective-permute-done.3 = bf16[240,128]{1,0:T(8,128)(2,1)S(1)} collective-permute-done((bf16[240,128]{1,0:T(8,128)(2,1)S(1)}, bf16[240,128]{1,0:T(8,128)(2,1)S(1)}, u32[]{:S(2)}, u32[]{:S(2)}) %collective-permute-start.3) | collective-permute-done | bytes 61472 | tf_op jit(solution)/shard_map/ppermute | solution.py:474
  19.6 2.3 %collective-permute-done.4 = bf16[240,128]{1,0:T(8,128)(2,1)S(1)} collective-permute-done((bf16[240,128]{1,0:T(8,128)(2,1)S(1)}, bf16[240,128]{1,0:T(8,128)(2,1)S(1)}, u32[]{:S(2)}, u32[]{:S(2)}) %collective-permute-start.4) | collective-permute-done | bytes 61472 | tf_op jit(solution)/shard_map/ppermute | solution.py:474
  22.0 2.3 %collective-permute-done.5 = bf16[240,128]{1,0:T(8,128)(2,1)S(1)} collective-permute-done((bf16[240,128]{1,0:T(8,128)(2,1)S(1)}, bf16[240,128]{1,0:T(8,128)(2,1)S(1)}, u32[]{:S(2)}, u32[]{:S(2)}) %collective-permute-start.5) | collective-permute-done | bytes 61472 | tf_op jit(solution)/shard_map/ppermute | solution.py:474
  24.4 1.6 %collective-permute-start.6 = (bf16[240,128]{1,0:T(8,128)(2,1)S(1)}, bf16[240,128]{1,0:T(8,128)(2,1)S(1)}, u32[]{:S(2)}, u32[]{:S(2)}) collective-permute-start(bf16[240,128]{1,0:T(8,128)(2,1)S(1)} %fusion.2), channel_id=1, source_target_pairs={{0,2},{1,3},{2,0},{3,1},{4,6},{5,7},{6,4},{7,5},{8,10},{9,11},{10,... | collective-permute-start | bytes 184328 | tf_op jit(solution)/shard_map/ppermute | solution.py:474
  26.0 2.6 %collective-permute-done.6 = bf16[240,128]{1,0:T(8,128)(2,1)S(1)} collective-permute-done((bf16[240,128]{1,0:T(8,128)(2,1)S(1)}, bf16[240,128]{1,0:T(8,128)(2,1)S(1)}, u32[]{:S(2)}, u32[]{:S(2)}) %collective-permute-start.6) | collective-permute-done | bytes 61472 | tf_op jit(solution)/shard_map/ppermute | solution.py:474
  28.7 2.7 %collective-permute-start.7 = (bf16[240,128]{1,0:T(8,128)(2,1)S(1)}, bf16[240,128]{1,0:T(8,128)(2,1)S(1)}, u32[]{:S(2)}, u32[]{:S(2)}) collective-permute-start(bf16[240,128]{1,0:T(8,128)(2,1)S(1)} %add_convert_fusion.1), channel_id=1, source_target_pairs={{0,4},{1,5},{2,6},{3,7},{4,0},{5,1},{6,2},{7,3},{8,12},{9,13},{10,... | collective-permute-start | bytes 184328 | tf_op jit(solution)/shard_map/ppermute | solution.py:474
  31.3 2.5 %collective-permute-done.7 = bf16[240,128]{1,0:T(8,128)(2,1)S(1)} collective-permute-done((bf16[240,128]{1,0:T(8,128)(2,1)S(1)}, bf16[240,128]{1,0:T(8,128)(2,1)S(1)}, u32[]{:S(2)}, u32[]{:S(2)}) %collective-permute-start.7) | collective-permute-done | bytes 61472 | tf_op jit(solution)/shard_map/ppermute | solution.py:474
  33.9 1.4 %collective-permute-start.8 = (bf16[240,128]{1,0:T(8,128)(2,1)S(1)}, bf16[240,128]{1,0:T(8,128)(2,1)S(1)}, u32[]{:S(2)}, u32[]{:S(2)}) collective-permute-start(bf16[240,128]{1,0:T(8,128)(2,1)S(1)} %get-tuple-element.39), channel_id=1, source_target_pairs={{0,1},{1,0},{2,3},{3,2},{4,5},{5,4},{6,7},{7,6},{8,9},{9,8},{10,11... | collective-permute-start | bytes 184328 | tf_op jit(solution)/shard_map/ppermute | solution.py:474
  35.3 0.4 collective-permute-start.9
  35.7 1.7 %collective-permute-start.10 = (bf16[240,128]{1,0:T(8,128)(2,1)S(1)}, bf16[240,128]{1,0:T(8,128)(2,1)S(1)}, u32[]{:S(2)}, u32[]{:S(2)}) collective-permute-start(bf16[240,128]{1,0:T(8,128)(2,1)S(1)} %get-tuple-element.39), channel_id=1, source_target_pairs={{0,17},{1,16},{2,19},{3,18},{4,21},{5,20},{6,23},{7,22},{8,25},{9,... | collective-permute-start | bytes 184328 | tf_op jit(solution)/shard_map/ppermute | solution.py:474
  37.5 0.7 %collective-permute-done.8 = bf16[240,128]{1,0:T(8,128)(2,1)S(1)} collective-permute-done((bf16[240,128]{1,0:T(8,128)(2,1)S(1)}, bf16[240,128]{1,0:T(8,128)(2,1)S(1)}, u32[]{:S(2)}, u32[]{:S(2)}) %collective-permute-start.8) | collective-permute-done | bytes 61472 | tf_op jit(solution)/shard_map/ppermute | solution.py:474
  38.2 1.3 %collective-permute-done.9 = bf16[240,128]{1,0:T(8,128)(2,1)S(1)} collective-permute-done((bf16[240,128]{1,0:T(8,128)(2,1)S(1)}, bf16[240,128]{1,0:T(8,128)(2,1)S(1)}, u32[]{:S(2)}, u32[]{:S(2)}) %collective-permute-start.9) | collective-permute-done | bytes 61472 | tf_op jit(solution)/shard_map/ppermute | solution.py:474
  39.6 1.3 %collective-permute-done.10 = bf16[240,128]{1,0:T(8,128)(2,1)S(1)} collective-permute-done((bf16[240,128]{1,0:T(8,128)(2,1)S(1)}, bf16[240,128]{1,0:T(8,128)(2,1)S(1)}, u32[]{:S(2)}, u32[]{:S(2)}) %collective-permute-start.10) | collective-permute-done | bytes 61472 | tf_op jit(solution)/shard_map/ppermute | solution.py:474
  40.9 0.1 collective-permute-start.11
  41.0 1.4 %shard_map.96 = (bf16[1,64,512]{2,1,0:T(8,128)(2,1)}, bf16[1,64,512]{2,1,0:T(8,128)(2,1)}) custom-call(bf16[8,64,128]{2,1,0:T(8,128)(2,1)S(1)} %get-tuple-element.29.rows_ref, bf16[8,80,128]{2,1,0:T(8,128)(2,1)S(1)} %get-tuple-element.30.delta_ref, bf16[2,240,64]{2,1,0:T(8,128)(2,1)S(1)} %get-tuple-element.31.pick_ref, ...), custom_call_target="tpu_custom_call" | custom-call | flops 1000000000 | bytes 2097152 | tf_op jit(solution)/shard_map/pallas_call | solution.py:431
  42.3 0.1 collective-permute-done.11
  42.4 1.1 %shard_map.97 = (f32[64,1728]{1,0:T(8,128)}, f32[64,1728]{1,0:T(8,128)}) custom-call(s32[1]{0:T(128)} %bitcast.7.refs_0_, bf16[5,192,128]{2,1,0:T(8,128)(2,1)S(1)} %bitcast.35, bf16[5,192,128]{2,1,0:T(8,128)(2,1)S(1)} %bitcast.38), custom_call_target="tpu_custom_call" | custom-call | tf_op jit(solution)/shard_map/pallas_call | solution.py:459
  (9 shorter events, 0.2 us)
Async XLA Ops:
  1.8 5.2 %collective-permute-start = (bf16[200,128]{1,0:T(8,128)(2,1)S(1)}, bf16[200,128]{1,0:T(8,128)(2,1)S(1)}, u32[]{:S(2)}, u32[]{:S(2)}) collective-permute-start(bf16[200,128]{1,0:T(8,128)(2,1)S(1)} %get-tuple-element.23), channel_id=1, source_target_pairs={{0,1},{1,0},{2,3},{3,2},{4,5},{5,4},{6,7},{7,6},{8,9},{9,8},{10,11... | collective-permute-start | bytes 153608 | tf_op jit(solution)/shard_map/ppermute | solution.py:524
  4.8 2.1 %collective-permute-start.1 = (bf16[200,128]{1,0:T(8,128)(2,1)S(1)}, bf16[200,128]{1,0:T(8,128)(2,1)S(1)}, u32[]{:S(2)}, u32[]{:S(2)}) collective-permute-start(bf16[200,128]{1,0:T(8,128)(2,1)S(1)} %get-tuple-element.24), channel_id=1, source_target_pairs={{1,2},{2,1},{3,4},{4,3},{5,6},{6,5},{9,10},{10,9},{11,12},{12,11},... | collective-permute-start | bytes 153608 | tf_op jit(solution)/shard_map/ppermute | solution.py:525
  10.7 1.6 %collective-permute-start.2 = (bf16[4,240,128]{2,1,0:T(8,128)(2,1)S(1)}, bf16[4,240,128]{2,1,0:T(8,128)(2,1)S(1)}, u32[]{:S(2)}, u32[]{:S(2)}) collective-permute-start(bf16[4,240,128]{2,1,0:T(8,128)(2,1)S(1)} %dynamic-slice_bitcast_fusion), channel_id=1, source_target_pairs={{0,8},{1,9},{2,10},{3,11},{4,12},{5,13},{6,14},{7,15},{8,0},{9,1},... | collective-permute-start | bytes 737288 | tf_op jit(solution)/shard_map/ppermute | solution.py:474
  12.4 7.3 %collective-permute-start.3 = (bf16[240,128]{1,0:T(8,128)(2,1)S(1)}, bf16[240,128]{1,0:T(8,128)(2,1)S(1)}, u32[]{:S(2)}, u32[]{:S(2)}) collective-permute-start(bf16[240,128]{1,0:T(8,128)(2,1)S(1)} %get-tuple-element.40), channel_id=1, source_target_pairs={{0,1},{1,0},{2,3},{3,2},{4,5},{5,4},{6,7},{7,6},{8,9},{9,8},{10,11... | collective-permute-start | bytes 184328 | tf_op jit(solution)/shard_map/ppermute | solution.py:474
  17.3 4.6 %collective-permute-start.4 = (bf16[240,128]{1,0:T(8,128)(2,1)S(1)}, bf16[240,128]{1,0:T(8,128)(2,1)S(1)}, u32[]{:S(2)}, u32[]{:S(2)}) collective-permute-start(bf16[240,128]{1,0:T(8,128)(2,1)S(1)} %get-tuple-element.42), channel_id=1, source_target_pairs={{0,16},{1,17},{2,18},{3,19},{4,20},{5,21},{6,22},{7,23},{8,24},{9,... | collective-permute-start | bytes 184328 | tf_op jit(solution)/shard_map/ppermute | solution.py:474
  19.2 5.1 %collective-permute-start.5 = (bf16[240,128]{1,0:T(8,128)(2,1)S(1)}, bf16[240,128]{1,0:T(8,128)(2,1)S(1)}, u32[]{:S(2)}, u32[]{:S(2)}) collective-permute-start(bf16[240,128]{1,0:T(8,128)(2,1)S(1)} %get-tuple-element.41), channel_id=1, source_target_pairs={{0,17},{1,16},{2,19},{3,18},{4,21},{5,20},{6,23},{7,22},{8,25},{9,... | collective-permute-start | bytes 184328 | tf_op jit(solution)/shard_map/ppermute | solution.py:474
  24.4 4.3 %collective-permute-start.6 = (bf16[240,128]{1,0:T(8,128)(2,1)S(1)}, bf16[240,128]{1,0:T(8,128)(2,1)S(1)}, u32[]{:S(2)}, u32[]{:S(2)}) collective-permute-start(bf16[240,128]{1,0:T(8,128)(2,1)S(1)} %fusion.2), channel_id=1, source_target_pairs={{0,2},{1,3},{2,0},{3,1},{4,6},{5,7},{6,4},{7,5},{8,10},{9,11},{10,... | collective-permute-start | bytes 184328 | tf_op jit(solution)/shard_map/ppermute | solution.py:474
  28.7 5.2 %collective-permute-start.7 = (bf16[240,128]{1,0:T(8,128)(2,1)S(1)}, bf16[240,128]{1,0:T(8,128)(2,1)S(1)}, u32[]{:S(2)}, u32[]{:S(2)}) collective-permute-start(bf16[240,128]{1,0:T(8,128)(2,1)S(1)} %add_convert_fusion.1), channel_id=1, source_target_pairs={{0,4},{1,5},{2,6},{3,7},{4,0},{5,1},{6,2},{7,3},{8,12},{9,13},{10,... | collective-permute-start | bytes 184328 | tf_op jit(solution)/shard_map/ppermute | solution.py:474
  33.9 4.3 %collective-permute-start.8 = (bf16[240,128]{1,0:T(8,128)(2,1)S(1)}, bf16[240,128]{1,0:T(8,128)(2,1)S(1)}, u32[]{:S(2)}, u32[]{:S(2)}) collective-permute-start(bf16[240,128]{1,0:T(8,128)(2,1)S(1)} %get-tuple-element.39), channel_id=1, source_target_pairs={{0,1},{1,0},{2,3},{3,2},{4,5},{5,4},{6,7},{7,6},{8,9},{9,8},{10,11... | collective-permute-start | bytes 184328 | tf_op jit(solution)/shard_map/ppermute | solution.py:474
  35.3 4.2 %collective-permute-start.9 = (bf16[240,128]{1,0:T(8,128)(2,1)S(1)}, bf16[240,128]{1,0:T(8,128)(2,1)S(1)}, u32[]{:S(2)}, u32[]{:S(2)}) collective-permute-start(bf16[240,128]{1,0:T(8,128)(2,1)S(1)} %get-tuple-element.39), channel_id=1, source_target_pairs={{0,16},{1,17},{2,18},{3,19},{4,20},{5,21},{6,22},{7,23},{8,24},{9,... | collective-permute-start | bytes 184328 | tf_op jit(solution)/shard_map/ppermute | solution.py:474
  35.7 5.1 %collective-permute-start.10 = (bf16[240,128]{1,0:T(8,128)(2,1)S(1)}, bf16[240,128]{1,0:T(8,128)(2,1)S(1)}, u32[]{:S(2)}, u32[]{:S(2)}) collective-permute-start(bf16[240,128]{1,0:T(8,128)(2,1)S(1)} %get-tuple-element.39), channel_id=1, source_target_pairs={{0,17},{1,16},{2,19},{3,18},{4,21},{5,20},{6,23},{7,22},{8,25},{9,... | collective-permute-start | bytes 184328 | tf_op jit(solution)/shard_map/ppermute | solution.py:474
  40.9 1.6 %collective-permute-start.11 = (bf16[4,240,128]{2,1,0:T(8,128)(2,1)S(1)}, bf16[4,240,128]{2,1,0:T(8,128)(2,1)S(1)}, u32[]{:S(2)}, u32[]{:S(2)}) collective-permute-start(bf16[4,240,128]{2,1,0:T(8,128)(2,1)S(1)} %bitcast_dynamic-update-slice_fusion), channel_id=1, source_target_pairs={{0,8},{1,9},{2,10},{3,11},{4,12},{5,13},{6,14},{7,15},{8,0},{9,1},... | collective-permute-start | bytes 737288 | tf_op jit(solution)/shard_map/ppermute | solution.py:474

commit v2 on v1

--- a/solution.py
+++ b/solution.py
@@ -25,11 +25,16 @@
 )
 TILES = len(PAIRS)
 KDIM = TILES * 2 * C
-LOW, OWN, HIGH = 0, 6, 16
-PLANES = 20
-SPLIT = 4
+SPLIT = 2
 WIDE = 4
 SPAN = 2
+
+PLANES = tuple(
+    p for k in range(WIDE) for p in ((-1, E - WIDE + k), (1, WIDE - 1 - k))
+) + ((-1, E), (1, -1), (0, -1), (0, E))
+REST = len(PLANES)
+RIMS = REST - 4
+BESIDE = slice((REST - 2) * E, REST * E)
 
 LIMIT = pltpu.CompilerParams(vmem_limit_bytes=24 << 20)
 HBM_SPEC = pl.BlockSpec(memory_space=pltpu.HBM)
@@ -50,8 +55,18 @@
     return lax.broadcasted_iota(jnp.int32, shape, len(shape) - 1) % (2 * C) < C
 
 
-def weight_kernel(w1_hbm, w2_hbm, f1_ref, f2_ref, b1_ref, b2_ref, w1_ref, w2_ref, sems):
-    fetch(((w1_hbm, w1_ref), (w2_hbm, w2_ref)), sems)
+def own_kernel(
+    w1_hbm, w2_hbm, feat_ref, f1_ref, f2_ref, b1_ref, b2_ref, q_ref, r_ref, w1_ref, w2_ref, sems
+):
+    copies = [
+        pltpu.make_async_copy(w1_hbm, w1_ref, sems.at[0]),
+        pltpu.make_async_copy(w2_hbm, w2_ref, sems.at[1]),
+    ]
+    for copy in copies:
+        copy.start()
+    put_interior(q_ref, 0, planes_of(feat_ref[0].astype(F32)))
+    for copy in copies:
+        copy.wait()
     zero = jnp.zeros((C, C), BF16)
     for w_ref, f_ref, b_ref in ((w1_ref, f1_ref, b1_ref), (w2_ref, f2_ref, b2_ref)):
         blocks = [w_ref[:, o * C : (o + 1) * C] for o in range(27)]
@@ -67,20 +82,35 @@
                 o = 26 - 3 * bc[0] - bc[1]
                 b_ref[rows, 0 : 2 * C] = jnp.concatenate([blocks[o], blocks[o - 9]], axis=1)
                 b_ref[rows, 2 * C : 4 * C] = jnp.concatenate([blocks[o - 18], blocks[o - 18]], axis=1)
-
-
-def prepare_weights(w1, w2):
+    w = f1_ref[...]
+    half = E // SPLIT
+    for y in range(0, E, half):
+        r = lax.dot_general(
+            q_ref[y : y + half].reshape(-1, KDIM), w, (((1,), (1,)), ((), ())), preferred_element_type=F32
+        )
+        r_ref[y : y + half] = r.reshape(half, FACE, 4 * C)
+
+
+def own_call(w1, w2, feat):
     fwd = jax.ShapeDtypeStruct((4 * C, KDIM), BF16)
     bwd = jax.ShapeDtypeStruct((KDIM, 4 * C), BF16)
+    w1, w2 = (pltpu.with_memory_space_constraint(v, pltpu.HBM) for v in (w1, w2))
     return pl.pallas_call(
-        weight_kernel,
-        out_shape=(fwd, fwd, bwd, bwd),
-        in_specs=[HBM_SPEC] * 2,
-        out_specs=(VMEM_SPEC,) * 4,
+        own_kernel,
+        out_shape=(
+            fwd,
+            fwd,
+            bwd,
+            bwd,
+            jax.ShapeDtypeStruct((E, FACE, KDIM), BF16),
+            jax.ShapeDtypeStruct((E, FACE, 4 * C), F32),
+        ),
+        in_specs=[HBM_SPEC] * 2 + [VMEM_SPEC],
+        out_specs=(VMEM_SPEC,) * 6,
         scratch_shapes=[pltpu.VMEM(w1.shape, BF16)] * 2 + [pltpu.SemaphoreType.DMA((2,))],
         compiler_params=LIMIT,
-        cost_estimate=pl.CostEstimate(flops=0, bytes_accessed=2 << 20, transcendentals=0),
-    )(*(pltpu.with_memory_space_constraint(v, pltpu.HBM) for v in (w1, w2)))
+        cost_estimate=pl.CostEstimate(flops=10**9, bytes_accessed=3 << 20, transcendentals=0),
+    )(w1, w2, feat)
 
 
 def rim_spread(first):
@@ -210,14 +240,25 @@
     return jnp.stack([v[:, y] for y in range(E)], axis=0)
 
 
-def x_taps(r, first, count):
-    here = slice(first, first + count)
-    prev = slice(first - 1, first + count - 1)
-    after = slice(first + 1, first + count + 1)
-    v0 = r[..., : 2 * C]
-    v1 = r[..., 2 * C :]
-    s = jnp.where(low_lanes((E, count, E, 2 * C)), v0[:, prev], v0[:, here])
-    return s + pltpu.roll(s, C, 3) + v1[:, after]
+def x_taps(own, rest, skip, planes):
+    def taps(names, lanes):
+        parts = []
+        for side, x in names:
+            inside = side == 0 and 0 <= x < E
+            source, k = (own, x) if inside else (rest, PLANES.index((side, x)) - skip)
+            parts.append(source[:, k : k + 1, :, lanes])
+        return jnp.concatenate(parts, axis=1)
+
+    low, high = slice(0, 2 * C), slice(2 * C, 4 * C)
+    prev = taps([(side, x - 1) for side, x in planes], low)
+    here = taps(planes, low)
+    after = taps([(side, x + 1) for side, x in planes], high)
+    s = jnp.where(low_lanes(here.shape), prev, here)
+    return s + pltpu.roll(s, C, 3) + after
+
+
+def planes_of(t):
+    return stack_x(jnp.transpose(jnp.concatenate([t, t], axis=0)).reshape(-1, E, 2 * C))
 
 
 def put_rows(out_ref, v):
@@ -259,21 +300,20 @@
         q_ref[y, rows, 8 * C : 10 * C] = z1[y + 2]
 
 
-def fill(q_ref, low, own, high, picks):
+def put_rest(q_ref, low, own, high, picks):
     low_pick, below_pick, above_pick, high_pick = picks
-    put_interior(q_ref, OWN, own)
-    put_interior(q_ref, LOW, low)
-    put_interior(q_ref, HIGH, high)
-    put_rims(
-        q_ref,
-        OWN - 2,
-        [rim_cells(low_pick, own[:, 0]), rim_cells(below_pick, low[:, -1])],
+    n = low.shape[1]
+    mixed = []
+    for k in range(n):
+        mixed += [low[:, k : k + 1], high[:, n - 1 - k : n - k]]
+    put_interior(q_ref, RIMS - 2 * n, jnp.concatenate(mixed, axis=1))
+    rims = (
+        rim_cells(low_pick, own[:, 0]),
+        rim_cells(high_pick, own[:, -1]),
+        rim_cells(below_pick, low[:, -1]),
+        rim_cells(above_pick, high[:, 0]),
     )
-    put_rims(
-        q_ref,
-        OWN + E,
-        [rim_cells(above_pick, high[:, 0]), rim_cells(high_pick, own[:, -1])],
-    )
+    put_rims(q_ref, RIMS, rims)
 
 
 def main_kernel(
@@ -286,13 +326,17 @@
     f1_ref,
     f2_ref,
     b2_ref,
+    q1_ref,
+    r1_ref,
     out_ref,
     grad_ref,
     delta_ref,
     pick_ref,
-    q1_ref,
     q2_ref,
     q3_ref,
+    rest1_ref,
+    rest2_ref,
+    rest3_ref,
 ):
     even = even_ref[0] == 1
     first = first_ref[...]
@@ -300,21 +344,19 @@
     upper = jnp.where(even, first, second).astype(F32)
     lower = jnp.where(even, second, first).astype(F32)
 
-    def planes(t):
-        return stack_x(jnp.transpose(jnp.concatenate([t, t], axis=0)).reshape(-1, E, 2 * C))
-
     def parts(packed):
         blocks = [packed[k * C : (k + 1) * C] for k in range((WIDE + SPAN) // 2)]
         codes = packed[len(blocks) * C :]
         f = jnp.concatenate(blocks[: WIDE // 2], axis=1)
         c = jnp.concatenate(blocks[WIDE // 2 :], axis=1)
-        return planes(f), planes(c), codes
+        return planes_of(f), planes_of(c), codes
 
     low_f, low_c, low_codes = parts(lower)
     high_f, high_c, high_codes = parts(upper)
     codes = codes_ref[...].astype(F32)
-    own_f = planes(feat_ref[0].astype(F32))
-    own_c = planes(cot_ref[0].astype(F32))
+    ends = jnp.concatenate([feat_ref[0, :, : 2 * C], feat_ref[0, :, -2 * C :]], axis=1)
+    own_f = planes_of(ends.astype(F32))
+    own_c = planes_of(cot_ref[0].astype(F32))
 
     picks = (
         pick_matrix(codes[0:1], low_codes[3:5]),
@@ -328,103 +370,107 @@
     def conv(q_ref, w, flipped=False, skip=0):
         dims = (((1,), (0 if flipped else 1,)), ((), ()))
         step = E // SPLIT
+        first = skip * E
         parts = []
         for y in range(0, E, step):
-            q = q_ref[y : y + step, skip * E : (PLANES - skip) * E, :].reshape(-1, KDIM)
-            r = lax.dot_general(q, w, dims, preferred_element_type=F32)
-            parts.append(r.reshape(step, PLANES - 2 * skip, E, 4 * C))
+            q = q_ref[y : y + step, first:, :]
+            count = q.shape[1] // E
+            r = lax.dot_general(q.reshape(-1, KDIM), w, dims, preferred_element_type=F32)
+            parts.append(r.reshape(step, count, E, 4 * C))
         return jnp.concatenate(parts, axis=0)
 
     def rounded(v):
         return v.astype(BF16).astype(F32)
 
-    def weight_gradient(which, q_ref, delta):
+    def weight_gradient(which, q_ref, rest_ref, delta):
+        def turned(d0, d1):
+            rows = d0.shape[0] * d0.shape[1] * E
+            d0 = jnp.transpose(d0.reshape(rows, 2 * C)).astype(BF16)
+            d1 = jnp.transpose(d1.reshape(rows, 2 * C))[:C].astype(BF16)
+            return jnp.concatenate([d0, d1], axis=0)
+
         zero = jnp.zeros((E, 1, E, 2 * C), F32)
-        d = jnp.concatenate([zero, zero, delta, zero, zero, zero], axis=1)
-        n = E + 4
-        before = jnp.concatenate([zero, d[:, : n - 1]], axis=1)
-        d0 = jnp.where(low_lanes((E, n, E, 2 * C)), d[:, 1 : n + 1], d[:, :n])
-        d1 = before
-        rows = E * n * E
-        d0 = jnp.transpose(d0.reshape(rows, 2 * C)).astype(BF16)
-        d1 = jnp.transpose(d1.reshape(rows, 2 * C))[:C].astype(BF16)
-        dt = jnp.concatenate([d0, d1], axis=0)
-        q = q_ref[:, (OWN - 2) * E : (OWN + E + 2) * E, :].reshape(rows, KDIM)
-        g = jnp.dot(dt, q, preferred_element_type=F32).astype(BF16)
-        for t in range(TILES):
-            grad_ref[which, t] = g[:, t * 2 * C : (t + 1) * 2 * C]
-
-    fill(q1_ref, low_f, own_f, high_f, picks)
-    r = conv(q1_ref, f1_ref[...])
-    pre_low = x_taps(r, LOW + 1, WIDE - 1)
-    pre_own = x_taps(r, OWN, E)
-    pre_high = x_taps(r, HIGH, WIDE - 1)
-    act = [rounded(v * sigmoid(v)) for v in (pre_low, pre_own, pre_high)]
-    pad_plane = jnp.zeros((E, 1, E, 2 * C), F32)
-    fill(
-        q2_ref,
-        jnp.concatenate([pad_plane, act[0]], axis=1),
-        act[1],
-        jnp.concatenate([act[2], pad_plane], axis=1),
-        picks,
+        up = jnp.concatenate([delta[:, 1:], zero], axis=1)
+        down = jnp.concatenate([zero, delta[:, :-1]], axis=1)
+        low = low_lanes(delta.shape)
+        own = turned(jnp.where(low, up, delta), down)
+        first = jnp.where(low[:, :1], delta[:, :1], 0.0)
+        ends = turned(
+            jnp.concatenate([first, zero], axis=1), jnp.concatenate([zero, delta[:, -1:]], axis=1)
+        )
+        g = jnp.dot(own, q_ref[...].reshape(-1, KDIM), preferred_element_type=F32)
+        g += jnp.dot(ends, rest_ref[:, BESIDE, :].reshape(-1, KDIM), preferred_element_type=F32)
+        rows = 3 * C
+        for t in range(TILES - 1):
+            grad_ref[which, t * rows : (t + 1) * rows, :] = g[:, t * 2 * C : (t + 1) * 2 * C].astype(BF16)
+        last = g[:, (TILES - 1) * 2 * C :]
+        packed = jnp.where(
+            low_lanes((rows // 2, 2 * C)), last[: rows // 2], pltpu.roll(last[rows // 2 :], C, 1)
+        )
+        grad_ref[which, (TILES - 1) * rows :, :] = packed.astype(BF16)
+
+    def near(side, count):
+        return [(-1, E - count + k) for k in range(count)] if side < 0 else [(1, k) for k in range(count)]
+
+    inside = [(0, x) for x in range(E)]
+
+    put_rest(rest1_ref, low_f, own_f, high_f, picks)
+    own = r1_ref[...].reshape(E, E, E, 4 * C)
+    rest = conv(rest1_ref, f1_ref[...])
+    pre_low, pre_own, pre_high = (
+        x_taps(own, rest, 0, p) for p in (near(-1, WIDE - 1), inside, near(1, WIDE - 1))
     )
-    r = conv(q2_ref, f2_ref[...])
-    second_own = x_taps(r, OWN, E)
+    act_low, act_own, act_high = (rounded(v * sigmoid(v)) for v in (pre_low, pre_own, pre_high))
+    put_interior(q2_ref, 0, act_own)
+    put_rest(rest2_ref, act_low, act_own, act_high, picks)
+    own, rest = conv(q2_ref, f2_ref[...]), conv(rest2_ref, f2_ref[...], False, 2)
+    second_own = x_taps(own, rest, 2, inside)
     out = second_own * sigmoid(second_own)
     out_ref[...] = out.reshape(E, FACE, 2 * C).astype(BF16)
-    second_low = x_taps(r, LOW + WIDE - SPAN, SPAN)
-    second_high = x_taps(r, HIGH, SPAN)
     delta_own = rounded(own_c * slope(second_own))
-    delta_low = rounded(low_c * slope(second_low))
-    delta_high = rounded(high_c * slope(second_high))
-    weight_gradient(1, q2_ref, delta_own)
-    pads = jnp.zeros((E, WIDE - SPAN, E, 2 * C), F32)
-    fill(
-        q3_ref,
-        jnp.concatenate([pads, delta_low], axis=1),
-        delta_own,
-        jnp.concatenate([delta_high, pads], axis=1),
-        picks,
-    )
-    skip = WIDE - SPAN
-    r = conv(q3_ref, b2_ref[...], True, skip)
-    first_own = rounded(x_taps(r, OWN - skip, E) * slope(pre_own))
-    first_low = rounded(x_taps(r, LOW + WIDE - 1 - skip, 1) * slope(pre_low[:, -1:]))
-    first_high = rounded(x_taps(r, HIGH - skip, 1) * slope(pre_high[:, :1]))
-    weight_gradient(0, q1_ref, first_own)
+    delta_low = rounded(low_c * slope(x_taps(own, rest, 2, near(-1, SPAN))))
+    delta_high = rounded(high_c * slope(x_taps(own, rest, 2, near(1, SPAN))))
+    put_interior(q3_ref, 0, delta_own)
+    put_rest(rest3_ref, delta_low, delta_own, delta_high, picks)
+    own, rest = conv(q3_ref, b2_ref[...], True), conv(rest3_ref, b2_ref[...], True, 4)
+    weight_gradient(1, q2_ref, rest2_ref, delta_own)
+    first_own = rounded(x_taps(own, rest, 4, inside) * slope(pre_own))
+    first_low = rounded(x_taps(own, rest, 4, near(-1, 1)) * slope(pre_low[:, -1:]))
+    first_high = rounded(x_taps(own, rest, 4, near(1, 1)) * slope(pre_high[:, :1]))
+    weight_gradient(0, q1_ref, rest1_ref, first_own)
     delta = jnp.concatenate([first_low, first_own, first_high], axis=1)
     delta_ref[...] = delta.reshape(E, (E + 2) * E, 2 * C).astype(BF16)
 
 
-def main_call(even, feat, cot, first, second, codes, f1, f2, b2):
-    q_shape = pltpu.VMEM((E, PLANES * E, KDIM), BF16)
+def main_call(even, feat, cot, first, second, codes, f1, f2, b2, q1, r1):
+    own_shape = pltpu.VMEM((E, FACE, KDIM), BF16)
+    rest_shape = pltpu.VMEM((E, REST * E, KDIM), BF16)
     return pl.pallas_call(
         main_kernel,
         out_shape=(
             jax.ShapeDtypeStruct((E, FACE, 2 * C), BF16),
-            jax.ShapeDtypeStruct((2, TILES, 3 * C, 2 * C), BF16),
+            jax.ShapeDtypeStruct((2, 27 * C // 2, 2 * C), BF16),
             jax.ShapeDtypeStruct((E, (E + 2) * E, 2 * C), BF16),
             jax.ShapeDtypeStruct((2, CELLS, FACE), BF16),
         ),
-        in_specs=[SMEM_SPEC] + [VMEM_SPEC] * 8,
+        in_specs=[SMEM_SPEC] + [VMEM_SPEC] * 10,
         out_specs=(VMEM_SPEC,) * 4,
-        scratch_shapes=[q_shape] * 3,
+        scratch_shapes=[own_shape] * 2 + [rest_shape] * 3,
         compiler_params=LIMIT,
         cost_estimate=pl.CostEstimate(flops=10**10, bytes_accessed=4 << 20, transcendentals=10**6),
-    )(even, feat, cot, first, second, codes, f1, f2, b2)
-
-
-def last_kernel(rows_ref, delta_ref, pick_ref, b1_ref, out_ref, grad_ref, q_ref):
+    )(even, feat, cot, first, second, codes, f1, f2, b2, q1, r1)
+
+
+def last_kernel(rows_ref, delta_ref, pick_ref, b1_ref, out_ref, grad_ref, q_ref, rim_ref):
     put_rows(out_ref, rows_ref[...].astype(F32).reshape(E, E, E, 2 * C))
     delta = delta_ref[...].astype(F32).reshape(E, E + 2, E, 2 * C)
-    put_interior(q_ref, 2, delta[:, 1 : E + 1])
-    below = rim_cells(pick_ref[0], delta[:, 0])
-    above = rim_cells(pick_ref[1], delta[:, E + 1])
-    put_rims(q_ref, 0, [below, below])
-    put_rims(q_ref, E + 2, [above, above])
-    q = q_ref[...].reshape(E * (E + 4) * E, KDIM)
-    r = jnp.dot(q, b1_ref[...], preferred_element_type=F32)
-    put_rows(grad_ref, x_taps(r.reshape(E, E + 4, E, 4 * C), 2, E))
+    put_interior(q_ref, 0, delta[:, 1 : E + 1])
+    put_rims(rim_ref, 0, (rim_cells(pick_ref[0], delta[:, 0]), rim_cells(pick_ref[1], delta[:, E + 1])))
+    b1 = b1_ref[...]
+    own = jnp.dot(q_ref[...].reshape(-1, KDIM), b1, preferred_element_type=F32)
+    rims = jnp.dot(rim_ref[...].reshape(-1, KDIM), b1, preferred_element_type=F32)
+    own, rims = own.reshape(E, E, E, 4 * C), rims.reshape(E, 2, E, 4 * C)
+    put_rows(grad_ref, x_taps(own, rims, REST - 2, [(0, x) for x in range(E)]))
 
 
 def last_call(rows, delta, pick, b1, shape):
@@ -433,36 +479,72 @@
         out_shape=(jax.ShapeDtypeStruct(shape, BF16),) * 2,
         in_specs=[VMEM_SPEC] * 4,
         out_specs=(VMEM_SPEC,) * 2,
-        scratch_shapes=[pltpu.VMEM((E, (E + 4) * E, KDIM), BF16)],
+        scratch_shapes=[pltpu.VMEM((E, FACE, KDIM), BF16), pltpu.VMEM((E, 2 * E, KDIM), BF16)],
         compiler_params=LIMIT,
         cost_estimate=pl.CostEstimate(flops=10**9, bytes_accessed=2 << 20, transcendentals=0),
     )(rows, delta, pick, b1)
 
 
-def finish_kernel(scale, flag_ref, mine_ref, theirs_ref, g1_ref, g2_ref):
-    swap = flag_ref[0] == 1
-    mine, theirs = mine_ref[...], theirs_ref[...]
-    for g_ref, one, two in ((g1_ref, mine, theirs), (g2_ref, theirs, mine)):
-        total = jnp.where(swap, two, one).astype(F32) * scale
-        for a in range(3):
-            at = {}
-            for t, pair in enumerate(PAIRS):
-                for h, bc in enumerate(pair):
-                    if bc is not None:
-                        at[3 * bc[0] + bc[1]] = total[t, a * C : (a + 1) * C, h * C : (h + 1) * C]
-            g_ref[:, 9 * a * C : 9 * (a + 1) * C] = jnp.concatenate([at[o] for o in range(9)], axis=1)
+def unpack(packed, scale, out_ref):
+    rows = 3 * C
+    v = packed.astype(F32) * scale
+    last = v[(TILES - 1) * rows :]
+    last = jnp.concatenate([last[:, :C], last[:, C:]], axis=0)
+    tiles = [v[t * rows : (t + 1) * rows] for t in range(TILES - 1)] + [last]
+    for a in range(3):
+        at = {}
+        for t, pair in enumerate(PAIRS):
+            for h, bc in enumerate(pair):
+                if bc is not None:
+                    at[3 * bc[0] + bc[1]] = tiles[t][a * C : (a + 1) * C, h * C : (h + 1) * C]
+        out_ref[:, 9 * a * C : 9 * (a + 1) * C] = jnp.concatenate([at[o] for o in range(9)], axis=1)
+
+
+def half_call(mine, scale):
+    def kernel(mine_ref, out_ref):
+        unpack(mine_ref[...], scale, out_ref)
+
+    return pl.pallas_call(
+        kernel,
+        out_shape=jax.ShapeDtypeStruct((C, 27 * C), F32),
+        in_specs=[VMEM_SPEC],
+        out_specs=VMEM_SPEC,
+        compiler_params=LIMIT,
+        cost_estimate=pl.CostEstimate(flops=0, bytes_accessed=1 << 20, transcendentals=0),
+    )(mine)
+
+
+def finish_kernel(scale, flag_ref, mine_ref, theirs_ref, g1_hbm, g2_hbm, other_ref, sems):
+    swapped = flag_ref[0] == 1
+
+    def put(mine_hbm, other_hbm):
+        first = pltpu.make_async_copy(mine_ref, mine_hbm, sems.at[0])
+        first.start()
+        unpack(theirs_ref[...], scale, other_ref)
+        second = pltpu.make_async_copy(other_ref, other_hbm, sems.at[1])
+        second.start()
+        first.wait()
+        second.wait()
+
+    @pl.when(swapped)
+    def _():
+        put(g2_hbm, g1_hbm)
+
+    @pl.when(jnp.logical_not(swapped))
+    def _():
+        put(g1_hbm, g2_hbm)
 
 
 def finish(flag, mine, theirs, scale):
     shape = jax.ShapeDtypeStruct((C, 27 * C), F32)
-    tiles = (TILES, 3 * C, 2 * C)
     return pl.pallas_call(
         lambda *refs: finish_kernel(scale, *refs),
         out_shape=(shape, shape),
         in_specs=[SMEM_SPEC] + [VMEM_SPEC] * 2,
-        out_specs=(VMEM_SPEC,) * 2,
+        out_specs=(HBM_SPEC,) * 2,
+        scratch_shapes=[pltpu.VMEM((C, 27 * C), F32), pltpu.SemaphoreType.DMA((2,))],
         compiler_params=LIMIT,
-    )(flag, mine.reshape(tiles), theirs.reshape(tiles))
+    )(flag, mine, theirs)
 
 
 def xor_permute(v, scene_bits, brick_bits):
@@ -501,14 +583,15 @@
     chip = (pick(parts, core).astype(F32) + other.astype(F32)).astype(BF16)
     moved = exchange([pick(chip, where ^ k) for k in (1, 2, 3)])
     plane = sum4(pick(chip, where), *moved).astype(BF16)
-    other = xor_permute(plane, 0, 2)
-    pair = (plane.astype(F32) + other.astype(F32)).astype(BF16)
-    other = xor_permute(pair, 0, 4)
-    whole = (pair.astype(F32) + other.astype(F32)).astype(BF16)
+    column = []
+    for k in (1, 2, 3):
+        column.append(xor_permute(plane, 0, 2 * k))
+    whole = sum4(plane, *column).astype(BF16)
     back = exchange([whole] * 3)
     mine = jnp.zeros(chip.shape, BF16)
     for k, piece in enumerate([whole] + back):
         mine = lax.dynamic_update_index_in_dim(mine, piece, where ^ k, 0)
+    mine = mine.reshape(v.shape[1:])
     theirs = xor_permute(mine, 1, 0)
     return core[None], mine, theirs
 
@@ -523,12 +606,13 @@
     between = [(i, ((i + 1) ^ 1) - 1) for i in range(1, bricks) if ((i + 1) ^ 1) - 1 < bricks]
     first = lax.ppermute(first, "brick", within)
     second = lax.ppermute(second, "brick", between)
-    f1, f2, b1, b2 = prepare_weights(first_weight.T, second_weight.T)
-
-    rows, grads, delta, pick = main_call(even, feat, cot, first, second, codes, f1, f2, b2)
+    f1, f2, b1, b2, q1, r1 = own_call(first_weight.T, second_weight.T, feat)
+
+    rows, grads, delta, pick = main_call(even, feat, cot, first, second, codes, f1, f2, b2, q1, r1)
     output, grad_input = last_call(rows, delta, pick, b1, feat.shape)
     flag, mine, theirs = all_sum(grads)
     scale = float(lax.axis_size("scene") * bricks * VOX) ** -0.5
+    mine = half_call(mine, scale)
     grad_first, grad_second = finish(flag, mine, theirs, scale)
     return jnp.swapaxes(output, 1, 2), jnp.swapaxes(grad_input, 1, 2), grad_first.T, grad_second.T
 

time: 43.8 us -> 44 us (level)
  waiting for transfers between devices: 15.4 us -> 15.9 us
    ppermute x10 -> x11, waiting for transfers between devices: 15.2 us -> 15.9 us  [xor_permute(): return lax.ppermute(v, BOTH, pairs)]
    pallas_call x1 -> x2, Pallas kernels: 1.26 us -> 1.72 us  [the longest x1 1.56 us: own_call(): pl.pallas_call(own_kernel, out_shape=(fwd, fwd, bwd, bwd, jax.ShapeDtypeS...]
    ppermute x10 -> x11, starting transfers between devices: 14.8 us -> 14.8 us  [xor_permute(): return lax.ppermute(v, BOTH, pairs)]
  transfers between devices with their start and end apart: 12 -> 13, of which waited for: 11 -> 10; matrix products, arithmetic and copies ran while one was open for 0% -> 0% of each run, Pallas kernels for 6% -> 7%
where the time goes in v2:
time: 44 us; the launch traced here: 43.8 us
  starting transfers between devices  18.6 us (42%)
  waiting for transfers between devices  15.9 us (36%)
  Pallas kernels  8.35 us (19%)
  between operations  0.78 us (2%)
    ppermute x11, waiting for transfers between devices, xor_permute(): return lax.ppermute(v, BOTH, pairs)  15.9 us
    ppermute x11, starting transfers between devices, xor_permute(): return lax.ppermute(v, BOTH, pairs)  14.8 us
    pallas_call x1, Pallas kernels, main_call(): pl.pallas_call(main_kernel, out_shape=(jax.ShapeDtypeStruct((E, FACE, 2 *...  3.32 us
    ppermute x1, starting transfers between devices, step(): first = lax.ppermute(first, 'brick', within)  3.08 us
    pallas_call x1, Pallas kernels, own_call(): pl.pallas_call(own_kernel, out_shape=(fwd, fwd, bwd, bwd, jax.ShapeDtypeS...  1.56 us
    pallas_call x1, Pallas kernels, last_call(): pl.pallas_call(last_kernel, out_shape=(jax.ShapeDtypeStruct(shape, BF16),...  1.26 us
    pallas_call x1, Pallas kernels, pack(): pl.pallas_call(pack_kernel, out_shape=(jax.ShapeDtypeStruct((rows, 2 * C)...  1.11 us
    pallas_call x1, Pallas kernels, finish(): pl.pallas_call(lambda *refs: finish_kernel(scale, *refs), out_shape=(shap...  0.95 us
  transfers between devices with their start and end apart: 13, of which 10 were waited for; matrix products, arithmetic and copies ran while one was open for 0% of the time, Pallas kernels for 7%

profile of v2, /device:TPU:0, one launch (start us, length us, event | category | flops | bytes accessed | tf_op | source)
XLA Modules:
  0.0 43.8 jit_solution(16190194617845479260)
XLA Ops:
  0.6 1.1 %shard_map.93 = (bf16[200,128]{1,0:T(8,128)(2,1)S(1)}, bf16[200,128]{1,0:T(8,128)(2,1)S(1)}, bf16[8,128]{1,0:T(8,128)(2,1)S(1)}, bf16[1,64,512]{2,1,0:T(8,128)(2,1)S(1)}, bf16[1,64,512]{2,1,0:T(8,128)(2,1)S(1)}) custom-call(s32[1]{0:T(128)} %bitcast.even_ref, bf16[1,64,512]{2,1,0:T(8,128)(2,1)} %bitcast.38, bf16[1,64,512]{2,1,0:T(8,128)(2,1)} %bitcast.39, ...), custom_call_target="tpu_custom_call" | custom-call | tf_op jit(solution)/shard_map/pallas_call | solution.py:197
  1.8 3.1 %collective-permute-start = (bf16[200,128]{1,0:T(8,128)(2,1)S(1)}, bf16[200,128]{1,0:T(8,128)(2,1)S(1)}, u32[]{:S(2)}, u32[]{:S(2)}) collective-permute-start(bf16[200,128]{1,0:T(8,128)(2,1)S(1)} %get-tuple-element.25), channel_id=1, source_target_pairs={{0,1},{1,0},{2,3},{3,2},{4,5},{5,4},{6,7},{7,6},{8,9},{9,8},{10,11... | collective-permute-start | bytes 153608 | tf_op jit(solution)/shard_map/ppermute | solution.py:607
  4.8 0.7 %collective-permute-start.1 = (bf16[200,128]{1,0:T(8,128)(2,1)S(1)}, bf16[200,128]{1,0:T(8,128)(2,1)S(1)}, u32[]{:S(2)}, u32[]{:S(2)}) collective-permute-start(bf16[200,128]{1,0:T(8,128)(2,1)S(1)} %get-tuple-element.26), channel_id=1, source_target_pairs={{1,2},{2,1},{3,4},{4,3},{5,6},{6,5},{9,10},{10,9},{11,12},{12,11},... | collective-permute-start | bytes 153608 | tf_op jit(solution)/shard_map/ppermute | solution.py:608
  5.5 1.6 %shard_map.94 = (bf16[256,640]{1,0:T(8,128)(2,1)S(1)}, bf16[256,640]{1,0:T(8,128)(2,1)S(1)}, bf16[640,256]{1,0:T(8,128)(2,1)S(1)}, bf16[640,256]{1,0:T(8,128)(2,...) custom-call(bf16[64,1728]{1,0:T(8,128)(2,1)} %bitcast.42, bf16[64,1728]{1,0:T(8,128)(2,1)} %bitcast.43, ...), custom_call_target="tpu_custom_call" | custom-call | flops 1000000000 | bytes 3145728 | tf_op jit(solution)/shard_map/pallas_call | solution.py:98
  7.1 0.0 collective-permute-done.first_ref
  7.1 0.0 collective-permute-done.1.second_ref
  7.1 3.3 %shard_map.95 = (bf16[8,64,128]{2,1,0:T(8,128)(2,1)S(1)}, bf16[2,864,128]{2,1,0:T(8,128)(2,1)S(1)}, bf16[8,80,128]{2,1,0:T(8,128)(2,1)S(1)}, bf16[2,240,64]{2,1,0:T(8,128)(2,1)S(1)}) custom-call(s32[1]{0:T(128)} %bitcast.even_ref, bf16[1,64,512]{2,1,0:T(8,128)(2,1)S(1)} %get-tuple-element.23.feat_ref, bf16[1,64,512]{2,1,0:T(8,128)(2,1)S(1)} %get-tuple-element.24.cot_ref, ...), custom_call_target="tpu_custom_call" | custom-call | flops 10000000000 | bytes 4194304 | tf_op jit(solution)/shard_map/pallas_call | solution.py:448
  10.4 0.1 collective-permute-start.2
  10.5 1.4 %collective-permute-done.2 = bf16[4,216,128]{2,1,0:T(8,128)(2,1)S(1)} collective-permute-done((bf16[4,216,128]{2,1,0:T(8,128)(2,1)S(1)}, bf16[4,216,128]{2,1,0:T(8,128)(2,1)S(1)}, u32[]{:S(2)}, u32[]{:S(2)}) %collective-permute-start.2) | collective-permute-done | bytes 221216 | tf_op jit(solution)/shard_map/ppermute | solution.py:556
  12.0 0.1 fusion
  12.1 4.8 %collective-permute-start.3 = (bf16[216,128]{1,0:T(8,128)(2,1)S(1)}, bf16[216,128]{1,0:T(8,128)(2,1)S(1)}, u32[]{:S(2)}, u32[]{:S(2)}) collective-permute-start(bf16[216,128]{1,0:T(8,128)(2,1)S(1)} %get-tuple-element.44), channel_id=1, source_target_pairs={{0,1},{1,0},{2,3},{3,2},{4,5},{5,4},{6,7},{7,6},{8,9},{9,8},{10,11... | collective-permute-start | bytes 165896 | tf_op jit(solution)/shard_map/ppermute | solution.py:556
  16.9 1.9 %collective-permute-start.4 = (bf16[216,128]{1,0:T(8,128)(2,1)S(1)}, bf16[216,128]{1,0:T(8,128)(2,1)S(1)}, u32[]{:S(2)}, u32[]{:S(2)}) collective-permute-start(bf16[216,128]{1,0:T(8,128)(2,1)S(1)} %get-tuple-element.46), channel_id=1, source_target_pairs={{0,16},{1,17},{2,18},{3,19},{4,20},{5,21},{6,22},{7,23},{8,24},{9,... | collective-permute-start | bytes 165896 | tf_op jit(solution)/shard_map/ppermute | solution.py:556
  18.8 0.0 collective-permute-start.5
  18.8 0.3 collective-permute-done.3
  19.1 2.3 %collective-permute-done.4 = bf16[216,128]{1,0:T(8,128)(2,1)S(1)} collective-permute-done((bf16[216,128]{1,0:T(8,128)(2,1)S(1)}, bf16[216,128]{1,0:T(8,128)(2,1)S(1)}, u32[]{:S(2)}, u32[]{:S(2)}) %collective-permute-start.4) | collective-permute-done | bytes 55328 | tf_op jit(solution)/shard_map/ppermute | solution.py:556
  21.4 2.4 %collective-permute-done.5 = bf16[216,128]{1,0:T(8,128)(2,1)S(1)} collective-permute-done((bf16[216,128]{1,0:T(8,128)(2,1)S(1)}, bf16[216,128]{1,0:T(8,128)(2,1)S(1)}, u32[]{:S(2)}, u32[]{:S(2)}) %collective-permute-start.5) | collective-permute-done | bytes 55328 | tf_op jit(solution)/shard_map/ppermute | solution.py:556
  23.9 1.6 %collective-permute-start.6 = (bf16[216,128]{1,0:T(8,128)(2,1)S(1)}, bf16[216,128]{1,0:T(8,128)(2,1)S(1)}, u32[]{:S(2)}, u32[]{:S(2)}) collective-permute-start(bf16[216,128]{1,0:T(8,128)(2,1)S(1)} %fusion.2), channel_id=1, source_target_pairs={{0,2},{1,3},{2,0},{3,1},{4,6},{5,7},{6,4},{7,5},{8,10},{9,11},{10,... | collective-permute-start | bytes 165896 | tf_op jit(solution)/shard_map/ppermute | solution.py:556
  25.5 2.2 %collective-permute-start.7 = (bf16[216,128]{1,0:T(8,128)(2,1)S(1)}, bf16[216,128]{1,0:T(8,128)(2,1)S(1)}, u32[]{:S(2)}, u32[]{:S(2)}) collective-permute-start(bf16[216,128]{1,0:T(8,128)(2,1)S(1)} %fusion.2), channel_id=1, source_target_pairs={{0,4},{1,5},{2,6},{3,7},{4,0},{5,1},{6,2},{7,3},{8,12},{9,13},{10,... | collective-permute-start | bytes 165896 | tf_op jit(solution)/shard_map/ppermute | solution.py:556
  27.7 0.6 %collective-permute-start.8 = (bf16[216,128]{1,0:T(8,128)(2,1)S(1)}, bf16[216,128]{1,0:T(8,128)(2,1)S(1)}, u32[]{:S(2)}, u32[]{:S(2)}) collective-permute-start(bf16[216,128]{1,0:T(8,128)(2,1)S(1)} %fusion.2), channel_id=1, source_target_pairs={{0,6},{1,7},{2,4},{3,5},{4,2},{5,3},{6,0},{7,1},{8,14},{9,15},{10,... | collective-permute-start | bytes 165896 | tf_op jit(solution)/shard_map/ppermute | solution.py:556
  28.3 0.3 collective-permute-done.6
  28.6 3.1 %collective-permute-done.7 = bf16[216,128]{1,0:T(8,128)(2,1)S(1)} collective-permute-done((bf16[216,128]{1,0:T(8,128)(2,1)S(1)}, bf16[216,128]{1,0:T(8,128)(2,1)S(1)}, u32[]{:S(2)}, u32[]{:S(2)}) %collective-permute-start.7) | collective-permute-done | bytes 55328 | tf_op jit(solution)/shard_map/ppermute | solution.py:556
  31.7 1.9 %collective-permute-done.8 = bf16[216,128]{1,0:T(8,128)(2,1)S(1)} collective-permute-done((bf16[216,128]{1,0:T(8,128)(2,1)S(1)}, bf16[216,128]{1,0:T(8,128)(2,1)S(1)}, u32[]{:S(2)}, u32[]{:S(2)}) %collective-permute-start.8) | collective-permute-done | bytes 55328 | tf_op jit(solution)/shard_map/ppermute | solution.py:556
  33.7 0.1 bitcast_dynamic-update-slice_fusion.3
  33.8 1.9 %collective-permute-start.9 = (bf16[216,128]{1,0:T(8,128)(2,1)S(1)}, bf16[216,128]{1,0:T(8,128)(2,1)S(1)}, u32[]{:S(2)}, u32[]{:S(2)}) collective-permute-start(bf16[216,128]{1,0:T(8,128)(2,1)S(1)} %get-tuple-element.43), channel_id=1, source_target_pairs={{0,1},{1,0},{2,3},{3,2},{4,5},{5,4},{6,7},{7,6},{8,9},{9,8},{10,11... | collective-permute-start | bytes 165896 | tf_op jit(solution)/shard_map/ppermute | solution.py:556
  35.7 0.5 %collective-permute-start.10 = (bf16[216,128]{1,0:T(8,128)(2,1)S(1)}, bf16[216,128]{1,0:T(8,128)(2,1)S(1)}, u32[]{:S(2)}, u32[]{:S(2)}) collective-permute-start(bf16[216,128]{1,0:T(8,128)(2,1)S(1)} %get-tuple-element.43), channel_id=1, source_target_pairs={{0,16},{1,17},{2,18},{3,19},{4,20},{5,21},{6,22},{7,23},{8,24},{9,... | collective-permute-start | bytes 165896 | tf_op jit(solution)/shard_map/ppermute | solution.py:556
  36.3 1.1 %collective-permute-start.11 = (bf16[216,128]{1,0:T(8,128)(2,1)S(1)}, bf16[216,128]{1,0:T(8,128)(2,1)S(1)}, u32[]{:S(2)}, u32[]{:S(2)}) collective-permute-start(bf16[216,128]{1,0:T(8,128)(2,1)S(1)} %get-tuple-element.43), channel_id=1, source_target_pairs={{0,17},{1,16},{2,19},{3,18},{4,21},{5,20},{6,23},{7,22},{8,25},{9,... | collective-permute-start | bytes 165896 | tf_op jit(solution)/shard_map/ppermute | solution.py:556
  37.3 0.7 %collective-permute-done.9 = bf16[216,128]{1,0:T(8,128)(2,1)S(1)} collective-permute-done((bf16[216,128]{1,0:T(8,128)(2,1)S(1)}, bf16[216,128]{1,0:T(8,128)(2,1)S(1)}, u32[]{:S(2)}, u32[]{:S(2)}) %collective-permute-start.9) | collective-permute-done | bytes 55328 | tf_op jit(solution)/shard_map/ppermute | solution.py:556
  38.0 1.9 %collective-permute-done.10 = bf16[216,128]{1,0:T(8,128)(2,1)S(1)} collective-permute-done((bf16[216,128]{1,0:T(8,128)(2,1)S(1)}, bf16[216,128]{1,0:T(8,128)(2,1)S(1)}, u32[]{:S(2)}, u32[]{:S(2)}) %collective-permute-start.10) | collective-permute-done | bytes 55328 | tf_op jit(solution)/shard_map/ppermute | solution.py:556
  39.9 1.4 %collective-permute-done.11 = bf16[216,128]{1,0:T(8,128)(2,1)S(1)} collective-permute-done((bf16[216,128]{1,0:T(8,128)(2,1)S(1)}, bf16[216,128]{1,0:T(8,128)(2,1)S(1)}, u32[]{:S(2)}, u32[]{:S(2)}) %collective-permute-start.11) | collective-permute-done | bytes 55328 | tf_op jit(solution)/shard_map/ppermute | solution.py:556
  41.3 0.1 collective-permute-start.12
  41.4 1.3 %shard_map.96 = (bf16[1,64,512]{2,1,0:T(8,128)(2,1)}, bf16[1,64,512]{2,1,0:T(8,128)(2,1)}) custom-call(bf16[8,64,128]{2,1,0:T(8,128)(2,1)S(1)} %get-tuple-element.33.rows_ref, bf16[8,80,128]{2,1,0:T(8,128)(2,1)S(1)} %get-tuple-element.34.delta_ref, bf16[2,240,64]{2,1,0:T(8,128)(2,1)S(1)} %get-tuple-element.35.pick_ref, ...), custom_call_target="tpu_custom_call" | custom-call | flops 1000000000 | bytes 2097152 | tf_op jit(solution)/shard_map/pallas_call | solution.py:477
  42.7 0.2 shard_map.97.refs_1_
  42.8 0.0 collective-permute-done.12.refs_2_
  42.9 0.9 %shard_map.98 = (f32[64,1728]{1,0:T(8,128)}, f32[64,1728]{1,0:T(8,128)}) custom-call(s32[1]{0:T(128)} %bitcast.7.refs_0_, f32[64,1728]{1,0:T(8,128)S(1)} %shard_map.97.refs_1_, bf16[864,128]{1,0:T(8,128)(2,1)S(1)} %collective-permute-done.12.refs_2_), custom_call_target="tpu_custom_call" | custom-call | tf_op jit(solution)/shard_map/pallas_call | solution.py:540
  (7 shorter events, 0.1 us)
Async XLA Ops:
  1.8 5.3 %collective-permute-start = (bf16[200,128]{1,0:T(8,128)(2,1)S(1)}, bf16[200,128]{1,0:T(8,128)(2,1)S(1)}, u32[]{:S(2)}, u32[]{:S(2)}) collective-permute-start(bf16[200,128]{1,0:T(8,128)(2,1)S(1)} %get-tuple-element.25), channel_id=1, source_target_pairs={{0,1},{1,0},{2,3},{3,2},{4,5},{5,4},{6,7},{7,6},{8,9},{9,8},{10,11... | collective-permute-start | bytes 153608 | tf_op jit(solution)/shard_map/ppermute | solution.py:607
  4.8 2.2 %collective-permute-start.1 = (bf16[200,128]{1,0:T(8,128)(2,1)S(1)}, bf16[200,128]{1,0:T(8,128)(2,1)S(1)}, u32[]{:S(2)}, u32[]{:S(2)}) collective-permute-start(bf16[200,128]{1,0:T(8,128)(2,1)S(1)} %get-tuple-element.26), channel_id=1, source_target_pairs={{1,2},{2,1},{3,4},{4,3},{5,6},{6,5},{9,10},{10,9},{11,12},{12,11},... | collective-permute-start | bytes 153608 | tf_op jit(solution)/shard_map/ppermute | solution.py:608
  10.4 1.5 %collective-permute-start.2 = (bf16[4,216,128]{2,1,0:T(8,128)(2,1)S(1)}, bf16[4,216,128]{2,1,0:T(8,128)(2,1)S(1)}, u32[]{:S(2)}, u32[]{:S(2)}) collective-permute-start(bf16[4,216,128]{2,1,0:T(8,128)(2,1)S(1)} %dynamic-slice_bitcast_fusion), channel_id=1, source_target_pairs={{0,8},{1,9},{2,10},{3,11},{4,12},{5,13},{6,14},{7,15},{8,0},{9,1},... | collective-permute-start | bytes 663560 | tf_op jit(solution)/shard_map/ppermute | solution.py:556
  12.1 7.0 %collective-permute-start.3 = (bf16[216,128]{1,0:T(8,128)(2,1)S(1)}, bf16[216,128]{1,0:T(8,128)(2,1)S(1)}, u32[]{:S(2)}, u32[]{:S(2)}) collective-permute-start(bf16[216,128]{1,0:T(8,128)(2,1)S(1)} %get-tuple-element.44), channel_id=1, source_target_pairs={{0,1},{1,0},{2,3},{3,2},{4,5},{5,4},{6,7},{7,6},{8,9},{9,8},{10,11... | collective-permute-start | bytes 165896 | tf_op jit(solution)/shard_map/ppermute | solution.py:556
  16.9 4.5 %collective-permute-start.4 = (bf16[216,128]{1,0:T(8,128)(2,1)S(1)}, bf16[216,128]{1,0:T(8,128)(2,1)S(1)}, u32[]{:S(2)}, u32[]{:S(2)}) collective-permute-start(bf16[216,128]{1,0:T(8,128)(2,1)S(1)} %get-tuple-element.46), channel_id=1, source_target_pairs={{0,16},{1,17},{2,18},{3,19},{4,20},{5,21},{6,22},{7,23},{8,24},{9,... | collective-permute-start | bytes 165896 | tf_op jit(solution)/shard_map/ppermute | solution.py:556
  18.8 5.1 %collective-permute-start.5 = (bf16[216,128]{1,0:T(8,128)(2,1)S(1)}, bf16[216,128]{1,0:T(8,128)(2,1)S(1)}, u32[]{:S(2)}, u32[]{:S(2)}) collective-permute-start(bf16[216,128]{1,0:T(8,128)(2,1)S(1)} %get-tuple-element.45), channel_id=1, source_target_pairs={{0,17},{1,16},{2,19},{3,18},{4,21},{5,20},{6,23},{7,22},{8,25},{9,... | collective-permute-start | bytes 165896 | tf_op jit(solution)/shard_map/ppermute | solution.py:556
  23.9 4.8 %collective-permute-start.6 = (bf16[216,128]{1,0:T(8,128)(2,1)S(1)}, bf16[216,128]{1,0:T(8,128)(2,1)S(1)}, u32[]{:S(2)}, u32[]{:S(2)}) collective-permute-start(bf16[216,128]{1,0:T(8,128)(2,1)S(1)} %fusion.2), channel_id=1, source_target_pairs={{0,2},{1,3},{2,0},{3,1},{4,6},{5,7},{6,4},{7,5},{8,10},{9,11},{10,... | collective-permute-start | bytes 165896 | tf_op jit(solution)/shard_map/ppermute | solution.py:556
  25.5 6.2 %collective-permute-start.7 = (bf16[216,128]{1,0:T(8,128)(2,1)S(1)}, bf16[216,128]{1,0:T(8,128)(2,1)S(1)}, u32[]{:S(2)}, u32[]{:S(2)}) collective-permute-start(bf16[216,128]{1,0:T(8,128)(2,1)S(1)} %fusion.2), channel_id=1, source_target_pairs={{0,4},{1,5},{2,6},{3,7},{4,0},{5,1},{6,2},{7,3},{8,12},{9,13},{10,... | collective-permute-start | bytes 165896 | tf_op jit(solution)/shard_map/ppermute | solution.py:556
  27.7 6.0 %collective-permute-start.8 = (bf16[216,128]{1,0:T(8,128)(2,1)S(1)}, bf16[216,128]{1,0:T(8,128)(2,1)S(1)}, u32[]{:S(2)}, u32[]{:S(2)}) collective-permute-start(bf16[216,128]{1,0:T(8,128)(2,1)S(1)} %fusion.2), channel_id=1, source_target_pairs={{0,6},{1,7},{2,4},{3,5},{4,2},{5,3},{6,0},{7,1},{8,14},{9,15},{10,... | collective-permute-start | bytes 165896 | tf_op jit(solution)/shard_map/ppermute | solution.py:556
  33.8 4.2 %collective-permute-start.9 = (bf16[216,128]{1,0:T(8,128)(2,1)S(1)}, bf16[216,128]{1,0:T(8,128)(2,1)S(1)}, u32[]{:S(2)}, u32[]{:S(2)}) collective-permute-start(bf16[216,128]{1,0:T(8,128)(2,1)S(1)} %get-tuple-element.43), channel_id=1, source_target_pairs={{0,1},{1,0},{2,3},{3,2},{4,5},{5,4},{6,7},{7,6},{8,9},{9,8},{10,11... | collective-permute-start | bytes 165896 | tf_op jit(solution)/shard_map/ppermute | solution.py:556
  35.7 4.2 %collective-permute-start.10 = (bf16[216,128]{1,0:T(8,128)(2,1)S(1)}, bf16[216,128]{1,0:T(8,128)(2,1)S(1)}, u32[]{:S(2)}, u32[]{:S(2)}) collective-permute-start(bf16[216,128]{1,0:T(8,128)(2,1)S(1)} %get-tuple-element.43), channel_id=1, source_target_pairs={{0,16},{1,17},{2,18},{3,19},{4,20},{5,21},{6,22},{7,23},{8,24},{9,... | collective-permute-start | bytes 165896 | tf_op jit(solution)/shard_map/ppermute | solution.py:556
  36.3 5.1 %collective-permute-start.11 = (bf16[216,128]{1,0:T(8,128)(2,1)S(1)}, bf16[216,128]{1,0:T(8,128)(2,1)S(1)}, u32[]{:S(2)}, u32[]{:S(2)}) collective-permute-start(bf16[216,128]{1,0:T(8,128)(2,1)S(1)} %get-tuple-element.43), channel_id=1, source_target_pairs={{0,17},{1,16},{2,19},{3,18},{4,21},{5,20},{6,23},{7,22},{8,25},{9,... | collective-permute-start | bytes 165896 | tf_op jit(solution)/shard_map/ppermute | solution.py:556
  41.3 1.5 %collective-permute-start.12 = (bf16[864,128]{1,0:T(8,128)(2,1)S(1)}, bf16[864,128]{1,0:T(8,128)(2,1)S(1)}, u32[]{:S(2)}, u32[]{:S(2)}) collective-permute-start(bf16[864,128]{1,0:T(8,128)(2,1)S(1)} %bitcast.34), channel_id=1, source_target_pairs={{0,8},{1,9},{2,10},{3,11},{4,12},{5,13},{6,14},{7,15},{8,0},{9,1},... | collective-permute-start | bytes 663560 | tf_op jit(solution)/shard_map/ppermute | solution.py:556

commit v3 on v2

--- a/solution.py
+++ b/solution.py
@@ -29,12 +29,18 @@
 WIDE = 4
 SPAN = 2
 
-PLANES = tuple(
-    p for k in range(WIDE) for p in ((-1, E - WIDE + k), (1, WIDE - 1 - k))
-) + ((-1, E), (1, -1), (0, -1), (0, E))
-REST = len(PLANES)
-RIMS = REST - 4
-BESIDE = slice((REST - 2) * E, REST * E)
+OWN = tuple((0, x) for x in range(E))
+SEAMS = ((-1, E), (1, -1), (0, -1), (0, E))
+
+
+def beyond(first):
+    return tuple(p for k in range(first, WIDE) for p in ((-1, E - WIDE + k), (1, WIDE - 1 - k)))
+
+
+INNER1, OUTER1 = OWN, beyond(0) + SEAMS
+INNER2, OUTER2 = OWN[1:-1], beyond(1) + SEAMS + (OWN[0], OWN[-1])
+INNER3, OUTER3 = OWN[2:-2], beyond(2) + SEAMS + (OWN[0], OWN[-1], OWN[1], OWN[-2])
+EDGE = OWN[:2] + OWN[-2:]
 
 LIMIT = pltpu.CompilerParams(vmem_limit_bytes=24 << 20)
 HBM_SPEC = pl.BlockSpec(memory_space=pltpu.HBM)
@@ -56,7 +62,26 @@
 
 
 def own_kernel(
-    w1_hbm, w2_hbm, feat_ref, f1_ref, f2_ref, b1_ref, b2_ref, q_ref, r_ref, w1_ref, w2_ref, sems
+    w1_hbm,
+    w2_hbm,
+    feat_ref,
+    cot_ref,
+    f1_ref,
+    f2_ref,
+    b1_ref,
+    b2_ref,
+    q1_ref,
+    q2_ref,
+    r1_ref,
+    r2_ref,
+    r3_ref,
+    slope_ref,
+    delta_ref,
+    out_ref,
+    q3_ref,
+    w1_ref,
+    w2_ref,
+    sems,
 ):
     copies = [
         pltpu.make_async_copy(w1_hbm, w1_ref, sems.at[0]),
@@ -64,7 +89,8 @@
     ]
     for copy in copies:
         copy.start()
-    put_interior(q_ref, 0, planes_of(feat_ref[0].astype(F32)))
+    put_interior(q1_ref, 0, planes_of(feat_ref[0].astype(F32)))
+    cot = planes_of(cot_ref[0, :, 2 * FACE : -2 * FACE].astype(F32))
     for copy in copies:
         copy.wait()
     zero = jnp.zeros((C, C), BF16)
@@ -82,18 +108,32 @@
                 o = 26 - 3 * bc[0] - bc[1]
                 b_ref[rows, 0 : 2 * C] = jnp.concatenate([blocks[o], blocks[o - 9]], axis=1)
                 b_ref[rows, 2 * C : 4 * C] = jnp.concatenate([blocks[o - 18], blocks[o - 18]], axis=1)
-    w = f1_ref[...]
-    half = E // SPLIT
-    for y in range(0, E, half):
-        r = lax.dot_general(
-            q_ref[y : y + half].reshape(-1, KDIM), w, (((1,), (1,)), ((), ())), preferred_element_type=F32
-        )
-        r_ref[y : y + half] = r.reshape(half, FACE, 4 * C)
-
-
-def own_call(w1, w2, feat):
+    r1 = conv(q1_ref, f1_ref[...])
+    r1_ref[...] = r1
+    pre = x_taps(((r1, INNER1),), INNER2)
+    slope_ref[...] = slope(pre)
+    put_interior(q2_ref, 0, rounded(pre * sigmoid(pre)))
+    r2 = conv(q2_ref, f2_ref[...])
+    r2_ref[...] = r2
+    pre = x_taps(((r2, INNER2),), INNER3)
+    out_ref[...] = (pre * sigmoid(pre)).astype(BF16)
+    delta = rounded(cot * slope(pre))
+    delta_ref[...] = delta
+    put_interior(q3_ref, 0, delta)
+    r3_ref[...] = conv(q3_ref, b2_ref[...], True)
+
+
+def own_call(w1, w2, feat, cot):
+    n1, n2, n3 = len(INNER1), len(INNER2), len(INNER3)
     fwd = jax.ShapeDtypeStruct((4 * C, KDIM), BF16)
     bwd = jax.ShapeDtypeStruct((KDIM, 4 * C), BF16)
+
+    def taps(n):
+        return jax.ShapeDtypeStruct((E, n, E, 4 * C), F32)
+
+    def values(n, dtype):
+        return jax.ShapeDtypeStruct((E, n, E, 2 * C), dtype)
+
     w1, w2 = (pltpu.with_memory_space_constraint(v, pltpu.HBM) for v in (w1, w2))
     return pl.pallas_call(
         own_kernel,
@@ -102,15 +142,23 @@
             fwd,
             bwd,
             bwd,
-            jax.ShapeDtypeStruct((E, FACE, KDIM), BF16),
-            jax.ShapeDtypeStruct((E, FACE, 4 * C), F32),
+            jax.ShapeDtypeStruct((E, n1 * E, KDIM), BF16),
+            jax.ShapeDtypeStruct((E, n2 * E, KDIM), BF16),
+            taps(n1),
+            taps(n2),
+            taps(n3),
+            values(n2, F32),
+            values(n3, F32),
+            values(n3, BF16),
         ),
-        in_specs=[HBM_SPEC] * 2 + [VMEM_SPEC],
-        out_specs=(VMEM_SPEC,) * 6,
-        scratch_shapes=[pltpu.VMEM(w1.shape, BF16)] * 2 + [pltpu.SemaphoreType.DMA((2,))],
+        in_specs=[HBM_SPEC] * 2 + [VMEM_SPEC] * 2,
+        out_specs=(VMEM_SPEC,) * 12,
+        scratch_shapes=[pltpu.VMEM((E, n3 * E, KDIM), BF16)]
+        + [pltpu.VMEM(w1.shape, BF16)] * 2
+        + [pltpu.SemaphoreType.DMA((2,))],
         compiler_params=LIMIT,
         cost_estimate=pl.CostEstimate(flops=10**9, bytes_accessed=3 << 20, transcendentals=0),
-    )(w1, w2, feat)
+    )(w1, w2, feat, cot)
 
 
 def rim_spread(first):
@@ -240,13 +288,29 @@
     return jnp.stack([v[:, y] for y in range(E)], axis=0)
 
 
-def x_taps(own, rest, skip, planes):
+def rounded(v):
+    return v.astype(BF16).astype(F32)
+
+
+def conv(q_ref, w, flipped=False):
+    dims = (((1,), (0 if flipped else 1,)), ((), ()))
+    step = E // SPLIT
+    parts = []
+    for y in range(0, E, step):
+        q = q_ref[y : y + step].reshape(-1, KDIM)
+        r = lax.dot_general(q, w, dims, preferred_element_type=F32)
+        parts.append(r.reshape(step, -1, E, 4 * C))
+    return jnp.concatenate(parts, axis=0)
+
+
+def x_taps(banks, planes):
     def taps(names, lanes):
         parts = []
-        for side, x in names:
-            inside = side == 0 and 0 <= x < E
-            source, k = (own, x) if inside else (rest, PLANES.index((side, x)) - skip)
-            parts.append(source[:, k : k + 1, :, lanes])
+        for name in names:
+            for r, held in banks:
+                if name in held:
+                    k = held.index(name)
+                    parts.append(r[:, k : k + 1, :, lanes])
         return jnp.concatenate(parts, axis=1)
 
     low, high = slice(0, 2 * C), slice(2 * C, 4 * C)
@@ -300,20 +364,22 @@
         q_ref[y, rows, 8 * C : 10 * C] = z1[y + 2]
 
 
-def put_rest(q_ref, low, own, high, picks):
+def put_outer(q_ref, low, ends, high, picks, count):
     low_pick, below_pick, above_pick, high_pick = picks
     n = low.shape[1]
     mixed = []
     for k in range(n):
         mixed += [low[:, k : k + 1], high[:, n - 1 - k : n - k]]
-    put_interior(q_ref, RIMS - 2 * n, jnp.concatenate(mixed, axis=1))
+    put_interior(q_ref, 0, jnp.concatenate(mixed, axis=1))
     rims = (
-        rim_cells(low_pick, own[:, 0]),
-        rim_cells(high_pick, own[:, -1]),
+        rim_cells(low_pick, ends[:, 0]),
+        rim_cells(high_pick, ends[:, 1]),
         rim_cells(below_pick, low[:, -1]),
         rim_cells(above_pick, high[:, 0]),
     )
-    put_rims(q_ref, RIMS, rims)
+    put_rims(q_ref, 2 * n, rims)
+    if count:
+        put_interior(q_ref, 2 * n + len(rims), ends[:, :count])
 
 
 def main_kernel(
@@ -327,16 +393,19 @@
     f2_ref,
     b2_ref,
     q1_ref,
+    q2_ref,
     r1_ref,
+    r2_ref,
+    r3_ref,
+    slope_ref,
+    inner_delta_ref,
     out_ref,
     grad_ref,
     delta_ref,
     pick_ref,
-    q2_ref,
-    q3_ref,
-    rest1_ref,
-    rest2_ref,
-    rest3_ref,
+    o1_ref,
+    o2_ref,
+    o3_ref,
 ):
     even = even_ref[0] == 1
     first = first_ref[...]
@@ -354,9 +423,14 @@
     low_f, low_c, low_codes = parts(lower)
     high_f, high_c, high_codes = parts(upper)
     codes = codes_ref[...].astype(F32)
-    ends = jnp.concatenate([feat_ref[0, :, : 2 * C], feat_ref[0, :, -2 * C :]], axis=1)
-    own_f = planes_of(ends.astype(F32))
-    own_c = planes_of(cot_ref[0].astype(F32))
+
+    def edge(ref):
+        return planes_of(jnp.concatenate([ref[0, :, : 2 * FACE], ref[0, :, -2 * FACE :]], axis=1).astype(F32))
+
+    def order(v, *names):
+        return jnp.concatenate([v[:, EDGE.index(n) : EDGE.index(n) + 1] for n in names], axis=1)
+
+    own_f, own_c = edge(feat_ref), edge(cot_ref)
 
     picks = (
         pick_matrix(codes[0:1], low_codes[3:5]),
@@ -367,39 +441,21 @@
     pick_ref[0] = picks[1]
     pick_ref[1] = picks[2]
 
-    def conv(q_ref, w, flipped=False, skip=0):
-        dims = (((1,), (0 if flipped else 1,)), ((), ()))
-        step = E // SPLIT
-        first = skip * E
-        parts = []
-        for y in range(0, E, step):
-            q = q_ref[y : y + step, first:, :]
-            count = q.shape[1] // E
-            r = lax.dot_general(q.reshape(-1, KDIM), w, dims, preferred_element_type=F32)
-            parts.append(r.reshape(step, count, E, 4 * C))
-        return jnp.concatenate(parts, axis=0)
-
-    def rounded(v):
-        return v.astype(BF16).astype(F32)
-
-    def weight_gradient(which, q_ref, rest_ref, delta):
-        def turned(d0, d1):
-            rows = d0.shape[0] * d0.shape[1] * E
+    def weight_gradient(which, banks, delta):
+        def plane(x):
+            return delta[:, x : x + 1] if 0 <= x < E else jnp.zeros((E, 1, E, 2 * C), F32)
+
+        g = 0.0
+        for q, names in banks:
+            rows = E * len(names) * E
+            up, here, down = (
+                jnp.concatenate([plane(x + k) for _, x in names], axis=1) for k in (1, 0, -1)
+            )
+            d0 = jnp.where(low_lanes(here.shape), up, here)
             d0 = jnp.transpose(d0.reshape(rows, 2 * C)).astype(BF16)
-            d1 = jnp.transpose(d1.reshape(rows, 2 * C))[:C].astype(BF16)
-            return jnp.concatenate([d0, d1], axis=0)
-
-        zero = jnp.zeros((E, 1, E, 2 * C), F32)
-        up = jnp.concatenate([delta[:, 1:], zero], axis=1)
-        down = jnp.concatenate([zero, delta[:, :-1]], axis=1)
-        low = low_lanes(delta.shape)
-        own = turned(jnp.where(low, up, delta), down)
-        first = jnp.where(low[:, :1], delta[:, :1], 0.0)
-        ends = turned(
-            jnp.concatenate([first, zero], axis=1), jnp.concatenate([zero, delta[:, -1:]], axis=1)
-        )
-        g = jnp.dot(own, q_ref[...].reshape(-1, KDIM), preferred_element_type=F32)
-        g += jnp.dot(ends, rest_ref[:, BESIDE, :].reshape(-1, KDIM), preferred_element_type=F32)
+            d1 = jnp.transpose(down.reshape(rows, 2 * C))[:C].astype(BF16)
+            d = jnp.concatenate([d0, d1], axis=0)
+            g += jnp.dot(d, q.reshape(rows, KDIM), preferred_element_type=F32)
         rows = 3 * C
         for t in range(TILES - 1):
             grad_ref[which, t * rows : (t + 1) * rows, :] = g[:, t * 2 * C : (t + 1) * 2 * C].astype(BF16)
@@ -410,79 +466,78 @@
         grad_ref[which, (TILES - 1) * rows :, :] = packed.astype(BF16)
 
     def near(side, count):
-        return [(-1, E - count + k) for k in range(count)] if side < 0 else [(1, k) for k in range(count)]
-
-    inside = [(0, x) for x in range(E)]
-
-    put_rest(rest1_ref, low_f, own_f, high_f, picks)
-    own = r1_ref[...].reshape(E, E, E, 4 * C)
-    rest = conv(rest1_ref, f1_ref[...])
-    pre_low, pre_own, pre_high = (
-        x_taps(own, rest, 0, p) for p in (near(-1, WIDE - 1), inside, near(1, WIDE - 1))
+        return tuple((-1, E - count + k) if side < 0 else (1, k) for k in range(count))
+
+    def from_plane(ref, names, first):
+        return ref[:, first * E :, :], names[first:]
+
+    put_outer(o1_ref, low_f, order(own_f, OWN[0], OWN[-1]), high_f, picks, 0)
+    banks = ((r1_ref[...], INNER1), (conv(o1_ref, f1_ref[...]), OUTER1))
+    pre_low, pre_ends, pre_high = (
+        x_taps(banks, p) for p in (near(-1, WIDE - 1), (OWN[0], OWN[-1]), near(1, WIDE - 1))
     )
-    act_low, act_own, act_high = (rounded(v * sigmoid(v)) for v in (pre_low, pre_own, pre_high))
-    put_interior(q2_ref, 0, act_own)
-    put_rest(rest2_ref, act_low, act_own, act_high, picks)
-    own, rest = conv(q2_ref, f2_ref[...]), conv(rest2_ref, f2_ref[...], False, 2)
-    second_own = x_taps(own, rest, 2, inside)
-    out = second_own * sigmoid(second_own)
-    out_ref[...] = out.reshape(E, FACE, 2 * C).astype(BF16)
-    delta_own = rounded(own_c * slope(second_own))
-    delta_low = rounded(low_c * slope(x_taps(own, rest, 2, near(-1, SPAN))))
-    delta_high = rounded(high_c * slope(x_taps(own, rest, 2, near(1, SPAN))))
-    put_interior(q3_ref, 0, delta_own)
-    put_rest(rest3_ref, delta_low, delta_own, delta_high, picks)
-    own, rest = conv(q3_ref, b2_ref[...], True), conv(rest3_ref, b2_ref[...], True, 4)
-    weight_gradient(1, q2_ref, rest2_ref, delta_own)
-    first_own = rounded(x_taps(own, rest, 4, inside) * slope(pre_own))
-    first_low = rounded(x_taps(own, rest, 4, near(-1, 1)) * slope(pre_low[:, -1:]))
-    first_high = rounded(x_taps(own, rest, 4, near(1, 1)) * slope(pre_high[:, :1]))
-    weight_gradient(0, q1_ref, rest1_ref, first_own)
+    act_low, act_ends, act_high = (rounded(v * sigmoid(v)) for v in (pre_low, pre_ends, pre_high))
+    put_outer(o2_ref, act_low, act_ends, act_high, picks, 2)
+    banks = ((r2_ref[...], INNER2), (conv(o2_ref, f2_ref[...]), OUTER2))
+    pre_edge = x_taps(banks, EDGE)
+    out_ref[...] = (pre_edge * sigmoid(pre_edge)).astype(BF16)
+    delta_edge = rounded(own_c * slope(pre_edge))
+    delta_low = rounded(low_c * slope(x_taps(banks, near(-1, SPAN))))
+    delta_high = rounded(high_c * slope(x_taps(banks, near(1, SPAN))))
+    put_outer(o3_ref, delta_low, order(delta_edge, OWN[0], OWN[-1], OWN[1], OWN[-2]), delta_high, picks, 4)
+    banks = ((r3_ref[...], INNER3), (conv(o3_ref, b2_ref[...], True), OUTER3))
+    delta_own = jnp.concatenate([delta_edge[:, :2], inner_delta_ref[...], delta_edge[:, 2:]], axis=1)
+    beside = len(OUTER2) - 4
+    weight_gradient(1, ((q2_ref[...], INNER2), from_plane(o2_ref, OUTER2, beside)), delta_own)
+    slope_ends = slope(pre_ends)
+    slopes = jnp.concatenate([slope_ends[:, :1], slope_ref[...], slope_ends[:, 1:]], axis=1)
+    first_own = rounded(x_taps(banks, OWN) * slopes)
+    first_low = rounded(x_taps(banks, near(-1, 1)) * slope(pre_low[:, -1:]))
+    first_high = rounded(x_taps(banks, near(1, 1)) * slope(pre_high[:, :1]))
+    beside = len(OUTER1) - 2
+    weight_gradient(0, ((q1_ref[...], INNER1), from_plane(o1_ref, OUTER1, beside)), first_own)
     delta = jnp.concatenate([first_low, first_own, first_high], axis=1)
     delta_ref[...] = delta.reshape(E, (E + 2) * E, 2 * C).astype(BF16)
 
 
-def main_call(even, feat, cot, first, second, codes, f1, f2, b2, q1, r1):
-    own_shape = pltpu.VMEM((E, FACE, KDIM), BF16)
-    rest_shape = pltpu.VMEM((E, REST * E, KDIM), BF16)
+def main_call(*operands):
+    outer = [pltpu.VMEM((E, len(names) * E, KDIM), BF16) for names in (OUTER1, OUTER2, OUTER3)]
     return pl.pallas_call(
         main_kernel,
         out_shape=(
-            jax.ShapeDtypeStruct((E, FACE, 2 * C), BF16),
+            jax.ShapeDtypeStruct((E, len(EDGE), E, 2 * C), BF16),
             jax.ShapeDtypeStruct((2, 27 * C // 2, 2 * C), BF16),
             jax.ShapeDtypeStruct((E, (E + 2) * E, 2 * C), BF16),
             jax.ShapeDtypeStruct((2, CELLS, FACE), BF16),
         ),
-        in_specs=[SMEM_SPEC] + [VMEM_SPEC] * 10,
+        in_specs=[SMEM_SPEC] + [VMEM_SPEC] * (len(operands) - 1),
         out_specs=(VMEM_SPEC,) * 4,
-        scratch_shapes=[own_shape] * 2 + [rest_shape] * 3,
+        scratch_shapes=outer,
         compiler_params=LIMIT,
         cost_estimate=pl.CostEstimate(flops=10**10, bytes_accessed=4 << 20, transcendentals=10**6),
-    )(even, feat, cot, first, second, codes, f1, f2, b2, q1, r1)
-
-
-def last_kernel(rows_ref, delta_ref, pick_ref, b1_ref, out_ref, grad_ref, q_ref, rim_ref):
-    put_rows(out_ref, rows_ref[...].astype(F32).reshape(E, E, E, 2 * C))
+    )(*operands)
+
+
+def last_kernel(edge_ref, inner_ref, delta_ref, pick_ref, b1_ref, out_ref, grad_ref, q_ref, rim_ref):
+    edge = edge_ref[...].astype(F32)
+    put_rows(out_ref, jnp.concatenate([edge[:, :2], inner_ref[...].astype(F32), edge[:, 2:]], axis=1))
     delta = delta_ref[...].astype(F32).reshape(E, E + 2, E, 2 * C)
     put_interior(q_ref, 0, delta[:, 1 : E + 1])
     put_rims(rim_ref, 0, (rim_cells(pick_ref[0], delta[:, 0]), rim_cells(pick_ref[1], delta[:, E + 1])))
-    b1 = b1_ref[...]
-    own = jnp.dot(q_ref[...].reshape(-1, KDIM), b1, preferred_element_type=F32)
-    rims = jnp.dot(rim_ref[...].reshape(-1, KDIM), b1, preferred_element_type=F32)
-    own, rims = own.reshape(E, E, E, 4 * C), rims.reshape(E, 2, E, 4 * C)
-    put_rows(grad_ref, x_taps(own, rims, REST - 2, [(0, x) for x in range(E)]))
-
-
-def last_call(rows, delta, pick, b1, shape):
+    banks = ((conv(q_ref, b1_ref[...], True), OWN), (conv(rim_ref, b1_ref[...], True), SEAMS[2:]))
+    put_rows(grad_ref, x_taps(banks, OWN))
+
+
+def last_call(edge, inner, delta, pick, b1, shape):
     return pl.pallas_call(
         last_kernel,
         out_shape=(jax.ShapeDtypeStruct(shape, BF16),) * 2,
-        in_specs=[VMEM_SPEC] * 4,
+        in_specs=[VMEM_SPEC] * 5,
         out_specs=(VMEM_SPEC,) * 2,
         scratch_shapes=[pltpu.VMEM((E, FACE, KDIM), BF16), pltpu.VMEM((E, 2 * E, KDIM), BF16)],
         compiler_params=LIMIT,
         cost_estimate=pl.CostEstimate(flops=10**9, bytes_accessed=2 << 20, transcendentals=0),
-    )(rows, delta, pick, b1)
+    )(edge, inner, delta, pick, b1)
 
 
 def unpack(packed, scale, out_ref):
@@ -606,10 +661,10 @@
     between = [(i, ((i + 1) ^ 1) - 1) for i in range(1, bricks) if ((i + 1) ^ 1) - 1 < bricks]
     first = lax.ppermute(first, "brick", within)
     second = lax.ppermute(second, "brick", between)
-    f1, f2, b1, b2, q1, r1 = own_call(first_weight.T, second_weight.T, feat)
-
-    rows, grads, delta, pick = main_call(even, feat, cot, first, second, codes, f1, f2, b2, q1, r1)
-    output, grad_input = last_call(rows, delta, pick, b1, feat.shape)
+    f1, f2, b1, b2, *own, inner_out = own_call(first_weight.T, second_weight.T, feat, cot)
+
+    edge_out, grads, delta, pick = main_call(even, feat, cot, first, second, codes, f1, f2, b2, *own)
+    output, grad_input = last_call(edge_out, inner_out, delta, pick, b1, feat.shape)
     flag, mine, theirs = all_sum(grads)
     scale = float(lax.axis_size("scene") * bricks * VOX) ** -0.5
     mine = half_call(mine, scale)

time: 44 us -> 43.8 us (level)
  starting transfers between devices: 18.6 us -> 17.8 us
  Pallas kernels: 8.35 us -> 8.93 us
    pallas_call x1, Pallas kernels: 1.56 us -> 2.34 us  [own_call(): pl.pallas_call(own_kernel, out_shape=(fwd, fwd, bwd, bwd, jax.ShapeDtypeS...]
    ppermute x11, starting transfers between devices: 14.8 us -> 14 us  [xor_permute(): return lax.ppermute(v, BOTH, pairs)]
  transfers between devices with their start and end apart: 13 -> 13, of which waited for: 10 -> 10; matrix products, arithmetic and copies ran while one was open for 0% -> 0% of each run, Pallas kernels for 7% -> 9%
where the time goes in v3:
time: 43.8 us; the launch traced here: 43.6 us
  starting transfers between devices  17.8 us (41%)
  waiting for transfers between devices  15.9 us (36%)
  Pallas kernels  8.93 us (20%)
  between operations  0.78 us (2%)
    ppermute x11, waiting for transfers between devices, xor_permute(): return lax.ppermute(v, BOTH, pairs)  15.9 us
    ppermute x11, starting transfers between devices, xor_permute(): return lax.ppermute(v, BOTH, pairs)  14 us
    pallas_call x1, Pallas kernels, main_call(): pl.pallas_call(main_kernel, out_shape=(jax.ShapeDtypeStruct((E, len(EDGE)...  3.1 us
    ppermute x1, starting transfers between devices, step(): first = lax.ppermute(first, 'brick', within)  3.08 us
    pallas_call x1, Pallas kernels, own_call(): pl.pallas_call(own_kernel, out_shape=(fwd, fwd, bwd, bwd, jax.ShapeDtypeS...  2.34 us
    pallas_call x1, Pallas kernels, last_call(): pl.pallas_call(last_kernel, out_shape=(jax.ShapeDtypeStruct(shape, BF16),...  1.28 us
    pallas_call x1, Pallas kernels, pack(): pl.pallas_call(pack_kernel, out_shape=(jax.ShapeDtypeStruct((rows, 2 * C)...  1.11 us
    pallas_call x1, Pallas kernels, finish(): pl.pallas_call(lambda *refs: finish_kernel(scale, *refs), out_shape=(shap...  0.95 us
  transfers between devices with their start and end apart: 13, of which 10 were waited for; matrix products, arithmetic and copies ran while one was open for 0% of the time, Pallas kernels for 9%

profile of v3, /device:TPU:0, one launch (start us, length us, event | category | flops | bytes accessed | tf_op | source)
XLA Modules:
  0.0 43.6 jit_solution(16707816562938384058)
XLA Ops:
  0.6 1.1 %shard_map.93 = (bf16[200,128]{1,0:T(8,128)(2,1)S(1)}, bf16[200,128]{1,0:T(8,128)(2,1)S(1)}, bf16[8,128]{1,0:T(8,128)(2,1)S(1)}, bf16[1,64,512]{2,1,0:T(8,128)(2,1)S(1)}, bf16[1,64,512]{2,1,0:T(8,128)(2,1)S(1)}) custom-call(s32[1]{0:T(128)} %bitcast.even_ref, bf16[1,64,512]{2,1,0:T(8,128)(2,1)} %bitcast.38, bf16[1,64,512]{2,1,0:T(8,128)(2,1)} %bitcast.39, ...), custom_call_target="tpu_custom_call" | custom-call | tf_op jit(solution)/shard_map/pallas_call | solution.py:245
  1.8 3.1 %collective-permute-start = (bf16[200,128]{1,0:T(8,128)(2,1)S(1)}, bf16[200,128]{1,0:T(8,128)(2,1)S(1)}, u32[]{:S(2)}, u32[]{:S(2)}) collective-permute-start(bf16[200,128]{1,0:T(8,128)(2,1)S(1)} %get-tuple-element.31), channel_id=1, source_target_pairs={{0,1},{1,0},{2,3},{3,2},{4,5},{5,4},{6,7},{7,6},{8,9},{9,8},{10,11... | collective-permute-start | bytes 153608 | tf_op jit(solution)/shard_map/ppermute | solution.py:662
  4.8 0.7 %collective-permute-start.1 = (bf16[200,128]{1,0:T(8,128)(2,1)S(1)}, bf16[200,128]{1,0:T(8,128)(2,1)S(1)}, u32[]{:S(2)}, u32[]{:S(2)}) collective-permute-start(bf16[200,128]{1,0:T(8,128)(2,1)S(1)} %get-tuple-element.32), channel_id=1, source_target_pairs={{1,2},{2,1},{3,4},{4,3},{5,6},{6,5},{9,10},{10,9},{11,12},{12,11},... | collective-permute-start | bytes 153608 | tf_op jit(solution)/shard_map/ppermute | solution.py:663
  5.5 2.3 %shard_map.94 = (bf16[256,640]{1,0:T(8,128)(2,1)S(1)}, bf16[256,640]{1,0:T(8,128)(2,1)S(1)}, bf16[640,256]{1,0:T(8,128)(2,1)S(1)}, bf16[640,256]{1,0:T(8,128)(2,...) custom-call(bf16[64,1728]{1,0:T(8,128)(2,1)} %bitcast.42, ...), custom_call_target="tpu_custom_call" | custom-call | flops 1000000000 | bytes 3145728 | tf_op jit(solution)/shard_map/pallas_call | solution.py:138
  7.8 0.0 collective-permute-done.first_ref
  7.9 0.0 collective-permute-done.1.second_ref
  7.9 3.1 %shard_map.95 = (bf16[8,4,8,128]{3,2,1,0:T(8,128)(2,1)S(1)}, bf16[2,864,128]{2,1,0:T(8,128)(2,1)S(1)}, bf16[8,80,128]{2,1,0:T(8,128)(2,1)S(1)}, bf16[2,240,64]{2,1,0:T(8,128)(2,1)S(1)}) custom-call(s32[1]{0:T(128)} %bitcast.even_ref, bf16[1,64,512]{2,1,0:T(8,128)(2,1)S(1)} %get-tuple-element.29.feat_ref, bf16[1,64,512]{2,1,0:T(8,128)(2,1)S(1)} %get-tuple-element.30.cot_ref, ...), custom_call_target="tpu_custom_call" | custom-call | flops 10000000000 | bytes 4194304 | tf_op jit(solution)/shard_map/pallas_call | solution.py:505
  11.0 0.1 collective-permute-start.2
  11.1 1.4 %collective-permute-done.2 = bf16[4,216,128]{2,1,0:T(8,128)(2,1)S(1)} collective-permute-done((bf16[4,216,128]{2,1,0:T(8,128)(2,1)S(1)}, bf16[4,216,128]{2,1,0:T(8,128)(2,1)S(1)}, u32[]{:S(2)}, u32[]{:S(2)}) %collective-permute-start.2) | collective-permute-done | bytes 221216 | tf_op jit(solution)/shard_map/ppermute | solution.py:611
  12.5 0.1 fusion
  12.6 4.3 %collective-permute-start.3 = (bf16[216,128]{1,0:T(8,128)(2,1)S(1)}, bf16[216,128]{1,0:T(8,128)(2,1)S(1)}, u32[]{:S(2)}, u32[]{:S(2)}) collective-permute-start(bf16[216,128]{1,0:T(8,128)(2,1)S(1)} %get-tuple-element.56), channel_id=1, source_target_pairs={{0,1},{1,0},{2,3},{3,2},{4,5},{5,4},{6,7},{7,6},{8,9},{9,8},{10,11... | collective-permute-start | bytes 165896 | tf_op jit(solution)/shard_map/ppermute | solution.py:611
  17.0 1.5 %collective-permute-start.4 = (bf16[216,128]{1,0:T(8,128)(2,1)S(1)}, bf16[216,128]{1,0:T(8,128)(2,1)S(1)}, u32[]{:S(2)}, u32[]{:S(2)}) collective-permute-start(bf16[216,128]{1,0:T(8,128)(2,1)S(1)} %get-tuple-element.58), channel_id=1, source_target_pairs={{0,16},{1,17},{2,18},{3,19},{4,20},{5,21},{6,22},{7,23},{8,24},{9,... | collective-permute-start | bytes 165896 | tf_op jit(solution)/shard_map/ppermute | solution.py:611
  18.5 0.0 collective-permute-start.5
  18.5 0.6 %collective-permute-done.3 = bf16[216,128]{1,0:T(8,128)(2,1)S(1)} collective-permute-done((bf16[216,128]{1,0:T(8,128)(2,1)S(1)}, bf16[216,128]{1,0:T(8,128)(2,1)S(1)}, u32[]{:S(2)}, u32[]{:S(2)}) %collective-permute-start.3) | collective-permute-done | bytes 55328 | tf_op jit(solution)/shard_map/ppermute | solution.py:611
  19.2 2.5 %collective-permute-done.4 = bf16[216,128]{1,0:T(8,128)(2,1)S(1)} collective-permute-done((bf16[216,128]{1,0:T(8,128)(2,1)S(1)}, bf16[216,128]{1,0:T(8,128)(2,1)S(1)}, u32[]{:S(2)}, u32[]{:S(2)}) %collective-permute-start.4) | collective-permute-done | bytes 55328 | tf_op jit(solution)/shard_map/ppermute | solution.py:611
  21.7 1.9 %collective-permute-done.5 = bf16[216,128]{1,0:T(8,128)(2,1)S(1)} collective-permute-done((bf16[216,128]{1,0:T(8,128)(2,1)S(1)}, bf16[216,128]{1,0:T(8,128)(2,1)S(1)}, u32[]{:S(2)}, u32[]{:S(2)}) %collective-permute-start.5) | collective-permute-done | bytes 55328 | tf_op jit(solution)/shard_map/ppermute | solution.py:611
  23.6 1.6 %collective-permute-start.6 = (bf16[216,128]{1,0:T(8,128)(2,1)S(1)}, bf16[216,128]{1,0:T(8,128)(2,1)S(1)}, u32[]{:S(2)}, u32[]{:S(2)}) collective-permute-start(bf16[216,128]{1,0:T(8,128)(2,1)S(1)} %fusion.2), channel_id=1, source_target_pairs={{0,2},{1,3},{2,0},{3,1},{4,6},{5,7},{6,4},{7,5},{8,10},{9,11},{10,... | collective-permute-start | bytes 165896 | tf_op jit(solution)/shard_map/ppermute | solution.py:611
  25.3 2.3 %collective-permute-start.7 = (bf16[216,128]{1,0:T(8,128)(2,1)S(1)}, bf16[216,128]{1,0:T(8,128)(2,1)S(1)}, u32[]{:S(2)}, u32[]{:S(2)}) collective-permute-start(bf16[216,128]{1,0:T(8,128)(2,1)S(1)} %fusion.2), channel_id=1, source_target_pairs={{0,4},{1,5},{2,6},{3,7},{4,0},{5,1},{6,2},{7,3},{8,12},{9,13},{10,... | collective-permute-start | bytes 165896 | tf_op jit(solution)/shard_map/ppermute | solution.py:611
  27.5 0.6 %collective-permute-start.8 = (bf16[216,128]{1,0:T(8,128)(2,1)S(1)}, bf16[216,128]{1,0:T(8,128)(2,1)S(1)}, u32[]{:S(2)}, u32[]{:S(2)}) collective-permute-start(bf16[216,128]{1,0:T(8,128)(2,1)S(1)} %fusion.2), channel_id=1, source_target_pairs={{0,6},{1,7},{2,4},{3,5},{4,2},{5,3},{6,0},{7,1},{8,14},{9,15},{10,... | collective-permute-start | bytes 165896 | tf_op jit(solution)/shard_map/ppermute | solution.py:611
  28.1 0.3 collective-permute-done.6
  28.4 3.2 %collective-permute-done.7 = bf16[216,128]{1,0:T(8,128)(2,1)S(1)} collective-permute-done((bf16[216,128]{1,0:T(8,128)(2,1)S(1)}, bf16[216,128]{1,0:T(8,128)(2,1)S(1)}, u32[]{:S(2)}, u32[]{:S(2)}) %collective-permute-start.7) | collective-permute-done | bytes 55328 | tf_op jit(solution)/shard_map/ppermute | solution.py:611
  31.5 2.0 %collective-permute-done.8 = bf16[216,128]{1,0:T(8,128)(2,1)S(1)} collective-permute-done((bf16[216,128]{1,0:T(8,128)(2,1)S(1)}, bf16[216,128]{1,0:T(8,128)(2,1)S(1)}, u32[]{:S(2)}, u32[]{:S(2)}) %collective-permute-start.8) | collective-permute-done | bytes 55328 | tf_op jit(solution)/shard_map/ppermute | solution.py:611
  33.5 0.1 bitcast_dynamic-update-slice_fusion.3
  33.6 1.9 %collective-permute-start.9 = (bf16[216,128]{1,0:T(8,128)(2,1)S(1)}, bf16[216,128]{1,0:T(8,128)(2,1)S(1)}, u32[]{:S(2)}, u32[]{:S(2)}) collective-permute-start(bf16[216,128]{1,0:T(8,128)(2,1)S(1)} %get-tuple-element.55), channel_id=1, source_target_pairs={{0,1},{1,0},{2,3},{3,2},{4,5},{5,4},{6,7},{7,6},{8,9},{9,8},{10,11... | collective-permute-start | bytes 165896 | tf_op jit(solution)/shard_map/ppermute | solution.py:611
  35.5 0.5 %collective-permute-start.10 = (bf16[216,128]{1,0:T(8,128)(2,1)S(1)}, bf16[216,128]{1,0:T(8,128)(2,1)S(1)}, u32[]{:S(2)}, u32[]{:S(2)}) collective-permute-start(bf16[216,128]{1,0:T(8,128)(2,1)S(1)} %get-tuple-element.55), channel_id=1, source_target_pairs={{0,16},{1,17},{2,18},{3,19},{4,20},{5,21},{6,22},{7,23},{8,24},{9,... | collective-permute-start | bytes 165896 | tf_op jit(solution)/shard_map/ppermute | solution.py:611
  36.0 1.1 %collective-permute-start.11 = (bf16[216,128]{1,0:T(8,128)(2,1)S(1)}, bf16[216,128]{1,0:T(8,128)(2,1)S(1)}, u32[]{:S(2)}, u32[]{:S(2)}) collective-permute-start(bf16[216,128]{1,0:T(8,128)(2,1)S(1)} %get-tuple-element.55), channel_id=1, source_target_pairs={{0,17},{1,16},{2,19},{3,18},{4,21},{5,20},{6,23},{7,22},{8,25},{9,... | collective-permute-start | bytes 165896 | tf_op jit(solution)/shard_map/ppermute | solution.py:611
  37.1 0.7 %collective-permute-done.9 = bf16[216,128]{1,0:T(8,128)(2,1)S(1)} collective-permute-done((bf16[216,128]{1,0:T(8,128)(2,1)S(1)}, bf16[216,128]{1,0:T(8,128)(2,1)S(1)}, u32[]{:S(2)}, u32[]{:S(2)}) %collective-permute-start.9) | collective-permute-done | bytes 55328 | tf_op jit(solution)/shard_map/ppermute | solution.py:611
  37.8 1.9 %collective-permute-done.10 = bf16[216,128]{1,0:T(8,128)(2,1)S(1)} collective-permute-done((bf16[216,128]{1,0:T(8,128)(2,1)S(1)}, bf16[216,128]{1,0:T(8,128)(2,1)S(1)}, u32[]{:S(2)}, u32[]{:S(2)}) %collective-permute-start.10) | collective-permute-done | bytes 55328 | tf_op jit(solution)/shard_map/ppermute | solution.py:611
  39.7 1.4 %collective-permute-done.11 = bf16[216,128]{1,0:T(8,128)(2,1)S(1)} collective-permute-done((bf16[216,128]{1,0:T(8,128)(2,1)S(1)}, bf16[216,128]{1,0:T(8,128)(2,1)S(1)}, u32[]{:S(2)}, u32[]{:S(2)}) %collective-permute-start.11) | collective-permute-done | bytes 55328 | tf_op jit(solution)/shard_map/ppermute | solution.py:611
  41.1 0.1 collective-permute-start.12
  41.2 1.3 %shard_map.96 = (bf16[1,64,512]{2,1,0:T(8,128)(2,1)}, bf16[1,64,512]{2,1,0:T(8,128)(2,1)}) custom-call(bf16[8,4,8,128]{3,2,1,0:T(8,128)(2,1)S(1)} %get-tuple-element.44.edge_ref, bf16[8,4,8,128]{3,2,1,0:T(8,128)(2,1)S(1)} %get-tuple-element.45.inner_ref, bf16[8,80,128]{2,1,0:T(8,128)(2,1)S(1)} %get-tuple-element.46.delta_ref, ...), custom_call_target="tpu_custom_call" | custom-call | flops 1000000000 | bytes 2097152 | tf_op jit(solution)/shard_map/pallas_call | solution.py:532
  42.5 0.2 shard_map.97.refs_1_
  42.6 0.0 collective-permute-done.12.refs_2_
  42.7 1.0 %shard_map.98 = (f32[64,1728]{1,0:T(8,128)}, f32[64,1728]{1,0:T(8,128)}) custom-call(s32[1]{0:T(128)} %bitcast.7.refs_0_, f32[64,1728]{1,0:T(8,128)S(1)} %shard_map.97.refs_1_, bf16[864,128]{1,0:T(8,128)(2,1)S(1)} %collective-permute-done.12.refs_2_), custom_call_target="tpu_custom_call" | custom-call | tf_op jit(solution)/shard_map/pallas_call | solution.py:595
  (7 shorter events, 0.1 us)
Async XLA Ops:
  1.8 6.1 %collective-permute-start = (bf16[200,128]{1,0:T(8,128)(2,1)S(1)}, bf16[200,128]{1,0:T(8,128)(2,1)S(1)}, u32[]{:S(2)}, u32[]{:S(2)}) collective-permute-start(bf16[200,128]{1,0:T(8,128)(2,1)S(1)} %get-tuple-element.31), channel_id=1, source_target_pairs={{0,1},{1,0},{2,3},{3,2},{4,5},{5,4},{6,7},{7,6},{8,9},{9,8},{10,11... | collective-permute-start | bytes 153608 | tf_op jit(solution)/shard_map/ppermute | solution.py:662
  4.8 3.0 %collective-permute-start.1 = (bf16[200,128]{1,0:T(8,128)(2,1)S(1)}, bf16[200,128]{1,0:T(8,128)(2,1)S(1)}, u32[]{:S(2)}, u32[]{:S(2)}) collective-permute-start(bf16[200,128]{1,0:T(8,128)(2,1)S(1)} %get-tuple-element.32), channel_id=1, source_target_pairs={{1,2},{2,1},{3,4},{4,3},{5,6},{6,5},{9,10},{10,9},{11,12},{12,11},... | collective-permute-start | bytes 153608 | tf_op jit(solution)/shard_map/ppermute | solution.py:663
  11.0 1.5 %collective-permute-start.2 = (bf16[4,216,128]{2,1,0:T(8,128)(2,1)S(1)}, bf16[4,216,128]{2,1,0:T(8,128)(2,1)S(1)}, u32[]{:S(2)}, u32[]{:S(2)}) collective-permute-start(bf16[4,216,128]{2,1,0:T(8,128)(2,1)S(1)} %dynamic-slice_bitcast_fusion), channel_id=1, source_target_pairs={{0,8},{1,9},{2,10},{3,11},{4,12},{5,13},{6,14},{7,15},{8,0},{9,1},... | collective-permute-start | bytes 663560 | tf_op jit(solution)/shard_map/ppermute | solution.py:611
  12.6 6.5 %collective-permute-start.3 = (bf16[216,128]{1,0:T(8,128)(2,1)S(1)}, bf16[216,128]{1,0:T(8,128)(2,1)S(1)}, u32[]{:S(2)}, u32[]{:S(2)}) collective-permute-start(bf16[216,128]{1,0:T(8,128)(2,1)S(1)} %get-tuple-element.56), channel_id=1, source_target_pairs={{0,1},{1,0},{2,3},{3,2},{4,5},{5,4},{6,7},{7,6},{8,9},{9,8},{10,11... | collective-permute-start | bytes 165896 | tf_op jit(solution)/shard_map/ppermute | solution.py:611
  17.0 4.7 %collective-permute-start.4 = (bf16[216,128]{1,0:T(8,128)(2,1)S(1)}, bf16[216,128]{1,0:T(8,128)(2,1)S(1)}, u32[]{:S(2)}, u32[]{:S(2)}) collective-permute-start(bf16[216,128]{1,0:T(8,128)(2,1)S(1)} %get-tuple-element.58), channel_id=1, source_target_pairs={{0,16},{1,17},{2,18},{3,19},{4,20},{5,21},{6,22},{7,23},{8,24},{9,... | collective-permute-start | bytes 165896 | tf_op jit(solution)/shard_map/ppermute | solution.py:611
  18.5 5.1 %collective-permute-start.5 = (bf16[216,128]{1,0:T(8,128)(2,1)S(1)}, bf16[216,128]{1,0:T(8,128)(2,1)S(1)}, u32[]{:S(2)}, u32[]{:S(2)}) collective-permute-start(bf16[216,128]{1,0:T(8,128)(2,1)S(1)} %get-tuple-element.57), channel_id=1, source_target_pairs={{0,17},{1,16},{2,19},{3,18},{4,21},{5,20},{6,23},{7,22},{8,25},{9,... | collective-permute-start | bytes 165896 | tf_op jit(solution)/shard_map/ppermute | solution.py:611
  23.6 4.7 %collective-permute-start.6 = (bf16[216,128]{1,0:T(8,128)(2,1)S(1)}, bf16[216,128]{1,0:T(8,128)(2,1)S(1)}, u32[]{:S(2)}, u32[]{:S(2)}) collective-permute-start(bf16[216,128]{1,0:T(8,128)(2,1)S(1)} %fusion.2), channel_id=1, source_target_pairs={{0,2},{1,3},{2,0},{3,1},{4,6},{5,7},{6,4},{7,5},{8,10},{9,11},{10,... | collective-permute-start | bytes 165896 | tf_op jit(solution)/shard_map/ppermute | solution.py:611
  25.3 6.2 %collective-permute-start.7 = (bf16[216,128]{1,0:T(8,128)(2,1)S(1)}, bf16[216,128]{1,0:T(8,128)(2,1)S(1)}, u32[]{:S(2)}, u32[]{:S(2)}) collective-permute-start(bf16[216,128]{1,0:T(8,128)(2,1)S(1)} %fusion.2), channel_id=1, source_target_pairs={{0,4},{1,5},{2,6},{3,7},{4,0},{5,1},{6,2},{7,3},{8,12},{9,13},{10,... | collective-permute-start | bytes 165896 | tf_op jit(solution)/shard_map/ppermute | solution.py:611
  27.5 6.0 %collective-permute-start.8 = (bf16[216,128]{1,0:T(8,128)(2,1)S(1)}, bf16[216,128]{1,0:T(8,128)(2,1)S(1)}, u32[]{:S(2)}, u32[]{:S(2)}) collective-permute-start(bf16[216,128]{1,0:T(8,128)(2,1)S(1)} %fusion.2), channel_id=1, source_target_pairs={{0,6},{1,7},{2,4},{3,5},{4,2},{5,3},{6,0},{7,1},{8,14},{9,15},{10,... | collective-permute-start | bytes 165896 | tf_op jit(solution)/shard_map/ppermute | solution.py:611
  33.6 4.2 %collective-permute-start.9 = (bf16[216,128]{1,0:T(8,128)(2,1)S(1)}, bf16[216,128]{1,0:T(8,128)(2,1)S(1)}, u32[]{:S(2)}, u32[]{:S(2)}) collective-permute-start(bf16[216,128]{1,0:T(8,128)(2,1)S(1)} %get-tuple-element.55), channel_id=1, source_target_pairs={{0,1},{1,0},{2,3},{3,2},{4,5},{5,4},{6,7},{7,6},{8,9},{9,8},{10,11... | collective-permute-start | bytes 165896 | tf_op jit(solution)/shard_map/ppermute | solution.py:611
  35.5 4.2 %collective-permute-start.10 = (bf16[216,128]{1,0:T(8,128)(2,1)S(1)}, bf16[216,128]{1,0:T(8,128)(2,1)S(1)}, u32[]{:S(2)}, u32[]{:S(2)}) collective-permute-start(bf16[216,128]{1,0:T(8,128)(2,1)S(1)} %get-tuple-element.55), channel_id=1, source_target_pairs={{0,16},{1,17},{2,18},{3,19},{4,20},{5,21},{6,22},{7,23},{8,24},{9,... | collective-permute-start | bytes 165896 | tf_op jit(solution)/shard_map/ppermute | solution.py:611
  36.0 5.1 %collective-permute-start.11 = (bf16[216,128]{1,0:T(8,128)(2,1)S(1)}, bf16[216,128]{1,0:T(8,128)(2,1)S(1)}, u32[]{:S(2)}, u32[]{:S(2)}) collective-permute-start(bf16[216,128]{1,0:T(8,128)(2,1)S(1)} %get-tuple-element.55), channel_id=1, source_target_pairs={{0,17},{1,16},{2,19},{3,18},{4,21},{5,20},{6,23},{7,22},{8,25},{9,... | collective-permute-start | bytes 165896 | tf_op jit(solution)/shard_map/ppermute | solution.py:611
  41.1 1.5 %collective-permute-start.12 = (bf16[864,128]{1,0:T(8,128)(2,1)S(1)}, bf16[864,128]{1,0:T(8,128)(2,1)S(1)}, u32[]{:S(2)}, u32[]{:S(2)}) collective-permute-start(bf16[864,128]{1,0:T(8,128)(2,1)S(1)} %bitcast.34), channel_id=1, source_target_pairs={{0,8},{1,9},{2,10},{3,11},{4,12},{5,13},{6,14},{7,15},{8,0},{9,1},... | collective-permute-start | bytes 663560 | tf_op jit(solution)/shard_map/ppermute | solution.py:611
